TPU v7x, 32 devices: a whole 2x2x4 slice. The times are simulated.
32 devices in a mesh: dop: 2 (over y), rng: 16 (over z, x, core).
Axes of the slice: x: 2, y: 2, z: 4, core: 2. Of those that a mesh axis runs over, the one named last changes fastest.
Arguments:
- radar_cube: bfloat16 [2, 128, 1024, 512], P(None, 'dop', 'rng'), may hold values from -40 to 40
- train_gates: int32 [2, 768], P('dop', 'rng'), may hold values from 0 to 63, as said below
- look_angles: int32 [2, 8], P('dop'), may hold values from 0 to 255
Outputs:
- filtered: float32 [2, 2, 8, 1024], P(None, 'dop', None, 'rng')
Inputs may be any that keep to these rules, and one draw needn't show every extreme that they name: `train_gates`: entries k * 48 to (k + 1) * 48 - 1 of a bin's row list in increasing order the gates of the k-th block of 64 consecutive range gates, counted from that block's first gate, that lie outside one run of 16 consecutive gates of the block.
All inputs are finite; a program needn't handle non-finite values.
Results may differ from a plain program's by a relative error of at most 0.014.
The roundings to bfloat16 on the way count: a program that leaves them out, or rounds other values in their place, can miss the bound.
Values may be sent and summed in bfloat16 or wider, within the bound.
No kernel may reach another device: no remote copies, remote signals or barrier semaphores. Data moves between devices by JAX's collectives and lax.ppermute only.
A program may use at most 64 MiB of HBM per device.

v0:
```python
import math

import jax
import jax.numpy as jnp
from jax import lax
from jax.sharding import PartitionSpec as P

P_SIZE = 128
NANG = 256


load_eps = 1e-05


def doppler_table(bin_count, pulses):
    bin_freq = jnp.arange(bin_count, dtype=jnp.int32) * (pulses // bin_count)
    pulse_index = jnp.arange(pulses, dtype=jnp.int32)
    phase = (bin_freq[:, None] * pulse_index[None, :] % pulses).astype(jnp.float32) * (
        2.0 * math.pi / pulses
    )
    cosine = jnp.cos(phase).astype(jnp.bfloat16)
    sine = jnp.sin(phase).astype(jnp.bfloat16)
    upper = jnp.concatenate([cosine, sine], 1)
    lower = jnp.concatenate([-sine, cosine], 1)
    return jnp.concatenate([upper, lower], 0)


def gram_terms(train_rows):
    real_part = train_rows[0]
    imag_part = train_rows[1]
    contract = (((0,), (0,)), ((), ()))
    stacked = jnp.concatenate([real_part, imag_part], 0)
    power_sum = lax.dot_general(stacked, stacked, contract, preferred_element_type=jnp.float32)
    left_rows = jnp.concatenate([real_part, -imag_part], 0)
    right_rows = jnp.concatenate([imag_part, real_part], 0)
    cross_sum = lax.dot_general(left_rows, right_rows, contract, preferred_element_type=jnp.float32)
    return (power_sum, cross_sum)


def solve_weights(power_sum, cross_sum, look_row, train_count, angle_count):
    channels = power_sum.shape[0]
    top_half = jnp.concatenate([power_sum, cross_sum], 1)
    bottom_half = jnp.concatenate([cross_sum.T, power_sum], 1)
    covariance = jnp.concatenate([top_half, bottom_half], 0) / train_count
    loading = load_eps * jnp.trace(covariance) / (2 * channels)
    covariance = covariance + loading * jnp.eye(2 * channels, dtype=jnp.float32)
    factor = jnp.linalg.cholesky(covariance)
    channel_index = jnp.arange(channels, dtype=jnp.int32)
    slope = 2 * look_row + 1 - angle_count
    modulus = channel_index[:, None] * slope[None, :] % (2 * angle_count)
    phase = modulus.astype(jnp.float32) * (math.pi / angle_count)
    steering = jnp.concatenate([jnp.cos(phase), jnp.sin(phase)], 0)
    whitened = jax.scipy.linalg.solve_triangular(factor, steering, lower=True)
    lengths = jnp.sqrt(jnp.sum(whitened * whitened, axis=0))
    weights = jax.scipy.linalg.solve_triangular(
        factor, whitened / lengths[None, :], trans=1, lower=True
    )
    return weights.astype(jnp.bfloat16)


def filter_gates(spectrum, weights):
    direct = jnp.concatenate([spectrum[0], spectrum[1]], 1)
    rotated = jnp.concatenate([-spectrum[1], spectrum[0]], 1)
    contract = (((0,), (1,)), ((), ()))
    real_out = lax.dot_general(weights, direct, contract, preferred_element_type=jnp.float32)
    imag_out = lax.dot_general(weights, rotated, contract, preferred_element_type=jnp.float32)
    return jnp.stack([real_out, imag_out])


def pack_terms(power_part, cross_part, lower_mask):
    return jnp.where(lower_mask, power_part, cross_part)


def unpack_terms(packed, row_index, col_index):
    lower_mask = row_index >= col_index
    lower_part = jnp.where(lower_mask, packed, 0.0)
    strict_lower = jnp.where(row_index > col_index, packed, 0.0)
    power_sum = lower_part + strict_lower.T
    upper_part = jnp.where(lower_mask, 0.0, packed)
    cross_sum = upper_part - upper_part.T
    return (power_sum, cross_sum)


def on_device(radar_cube, train_gates, look_angles):
    dop_count = lax.axis_size("dop")
    rng_count = lax.axis_size("rng")
    bin_local = train_gates.shape[0]
    bin_count = dop_count * bin_local
    dft_table = doppler_table(bin_count, P_SIZE)
    norm_scale = 1.0 / math.sqrt(P_SIZE)
    segment = lax.all_to_all(radar_cube, "dop", split_axis=2, concat_axis=1, tiled=True)
    flattened = segment.reshape(2 * P_SIZE, -1)
    spectral = (
        jnp.dot(dft_table, flattened, preferred_element_type=jnp.float32) * norm_scale
    ).astype(jnp.bfloat16)
    spectral = spectral.reshape(2, bin_count, segment.shape[2], segment.shape[3])
    binned = lax.all_to_all(spectral, "dop", split_axis=1, concat_axis=2, tiled=True)
    channels = binned.shape[3]
    train_count = train_gates.shape[1] * rng_count
    row_index = lax.broadcasted_iota(jnp.int32, (channels, channels), 0)
    col_index = lax.broadcasted_iota(jnp.int32, (channels, channels), 1)
    lower_mask = row_index >= col_index
    rows = jnp.take(binned[:, 0], train_gates[0], axis=1)
    power_part, cross_part = gram_terms(rows)
    packed_all = jnp.stack([pack_terms(power_part, cross_part, lower_mask)])
    summed = lax.psum(packed_all, "rng")

    def unpack_one(packed):
        return unpack_terms(packed, row_index, col_index)

    power_all, cross_all = jax.vmap(unpack_one)(summed)

    def solve_one(inputs):
        return solve_weights(inputs[0], inputs[1], inputs[2], train_count, NANG)

    weights_all = lax.map(solve_one, (power_all, cross_all, look_angles))
    outputs = [filter_gates(binned[:, 0], weights_all[0])]
    return jnp.stack(outputs, 1)


def solution(mesh):
    placed = (P(None, "dop", "rng", None), P("dop", "rng"), P("dop", None))
    return jax.shard_map(
        on_device,
        mesh=mesh,
        in_specs=placed,
        out_specs=P(None, "dop", None, "rng"),
        check_vma=False,
    )
```

profile of v0, /device:TPU:0, one launch (start us, length us, event | category | flops | bytes accessed | tf_op | source)
XLA Modules:
  0.0 629.8 jit_solution(5859860382280964349)
XLA Ops:
  6.5 11.3 %copy.107 = bf16[2,64,64,512]{3,1,0,2:T(8,128)(2,1)} copy(bf16[2,64,64,512]{3,2,1,0:T(8,128)(2,1)} %param.3) | data formatting | bytes 16777216 | tf_op args[0]
  17.9 7.6 %all-to-all-start = ((bf16[2,64,64,512]{3,1,0,2:T(8,128)(2,1)}), bf16[2,64,64,512]{3,1,0,2:T(8,128)(2,1)}, u32[]{:S(2)}, u32[]{:S(2)}) async-start(bf16[2,64,64,512]{3,1,0,2:T(8,128)(2,1)} %copy.107), calls=%async_computation | async-start | bytes 16777216 | tf_op jit(solution)/shard_map/all_to_all | solution.py:91
  26.4 92.9 %all-to-all-done = bf16[2,64,64,512]{3,1,0,2:T(8,128)(2,1)} async-done(((bf16[2,64,64,512]{3,1,0,2:T(8,128)(2,1)}), bf16[2,64,64,512]{3,1,0,2:T(8,128)(2,1)}, u32[]{:S(2)}, u32[]{:S(2)}) %all-to-all-start) | async-done | bytes 8388640 | tf_op jit(solution)/shard_map/all_to_all | solution.py:91
  119.4 11.4 %copy.108 = bf16[2,64,2,32,512]{4,3,1,2,0:T(8,128)(2,1)} copy(bf16[2,64,2,32,512]{4,1,0,3,2:T(8,128)(2,1)} %bitcast.1) | data formatting | bytes 16777216 | tf_op jit(solution)/shard_map/all_to_all | solution.py:91
  130.8 15.5 %copy.155 = bf16[32,8,32,512]{3,1,2,0:T(8,128)(2,1)} copy(bf16[32,8,32,512]{3,2,1,0:T(8,128)(2,1)} %bitcast.183) | data formatting | bytes 16777216
  146.3 4.6 fusion
  151.6 3.4 all-to-all-start.1
  155.0 4.4 all-to-all-done.1
  162.4 94.3 %all-reduce.3.cloned.1.call-done = f32[1,512,512]{2,1,0:T(8,128)} async-done(((f32[1,512,512]{2,1,0:T(8,128)}), f32[1,512,512]{2,1,0:T(8,128)}) %all-reduce.3.cloned.1.call-update) | async-done | bytes 1048592 | tf_op jit(solution)/shard_map/psum | solution.py:106
  260.9 3.3 fusion.11
  269.9 5.5 copy.117
  275.4 3.2 fusion.1
  280.6 11.7 %cholesky.222 = f32[128,128]{1,0:T(8,128)S(1)} custom-call(f32[128,128]{1,0:T(8,128)S(1)} %cholesky.577), custom_call_target="Cholesky" | custom-call | tf_op jit(solution)/shard_map/while/body/eval_jaxpr/jit(cholesky)/cholesky | solution.py:47
  292.3 9.8 %custom-call.82 = f32[1,128,128]{1,2,0:T(8,128)S(1)} custom-call(f32[1,128,128]{2,1,0:T(8,128)S(1)} %get-tuple-element.79), custom_call_target="InvertDiagBlocksLowerTriangular" | custom-call | tf_op jit(solution)/shard_map/while/body/eval_jaxpr/jit(cholesky)/cholesky | solution.py:47
  305.3 11.7 %cholesky.243 = f32[128,128]{1,0:T(8,128)S(1)} custom-call(f32[128,128]{1,0:T(8,128)S(1)} %cholesky.581), custom_call_target="Cholesky" | custom-call | tf_op jit(solution)/shard_map/while/body/eval_jaxpr/jit(cholesky)/cholesky | solution.py:47
  317.8 9.8 %custom-call.83 = f32[1,128,128]{1,2,0:T(8,128)S(1)} custom-call(f32[1,128,128]{2,1,0:T(8,128)S(1)} %get-tuple-element.77), custom_call_target="InvertDiagBlocksLowerTriangular" | custom-call | tf_op jit(solution)/shard_map/while/body/eval_jaxpr/jit(cholesky)/cholesky | solution.py:47
  333.1 11.7 %cholesky.466 = f32[128,128]{1,0:T(8,128)S(1)} custom-call(f32[128,128]{1,0:T(8,128)S(1)} %cholesky.586), custom_call_target="Cholesky" | custom-call | tf_op jit(solution)/shard_map/while/body/eval_jaxpr/jit(cholesky)/cholesky | solution.py:47
  345.6 9.8 %custom-call.84 = f32[1,128,128]{1,2,0:T(8,128)S(1)} custom-call(f32[1,128,128]{2,1,0:T(8,128)S(1)} %get-tuple-element.75), custom_call_target="InvertDiagBlocksLowerTriangular" | custom-call | tf_op jit(solution)/shard_map/while/body/eval_jaxpr/jit(cholesky)/cholesky | solution.py:47
  356.7 3.3 convolution_subtract_fusion.2
  360.0 11.7 %cholesky.485 = f32[128,128]{1,0:T(8,128)S(1)} custom-call(f32[128,128]{1,0:T(8,128)S(1)} %cholesky.591), custom_call_target="Cholesky" | custom-call | tf_op jit(solution)/shard_map/while/body/eval_jaxpr/jit(cholesky)/cholesky | solution.py:47
  372.5 9.8 %custom-call.85 = f32[1,128,128]{1,2,0:T(8,128)S(1)} custom-call(f32[1,128,128]{2,1,0:T(8,128)S(1)} %get-tuple-element.73), custom_call_target="InvertDiagBlocksLowerTriangular" | custom-call | tf_op jit(solution)/shard_map/while/body/eval_jaxpr/jit(cholesky)/cholesky | solution.py:47
  383.4 3.1 convolution_subtract_fusion.3
  386.6 11.9 %cholesky.504 = f32[128,128]{1,0:T(8,128)S(1)} custom-call(f32[128,128]{1,0:T(8,128)S(1)} %cholesky.596), custom_call_target="Cholesky" | custom-call | tf_op jit(solution)/shard_map/while/body/eval_jaxpr/jit(cholesky)/cholesky | solution.py:47
  399.3 9.8 %custom-call.86 = f32[1,128,128]{1,2,0:T(8,128)S(1)} custom-call(f32[1,128,128]{2,1,0:T(8,128)S(1)} %get-tuple-element.71), custom_call_target="InvertDiagBlocksLowerTriangular" | custom-call | tf_op jit(solution)/shard_map/while/body/eval_jaxpr/jit(cholesky)/cholesky | solution.py:47
  413.3 11.7 %cholesky.524 = f32[128,128]{1,0:T(8,128)S(1)} custom-call(f32[128,128]{1,0:T(8,128)S(1)} %cholesky.601), custom_call_target="Cholesky" | custom-call | tf_op jit(solution)/shard_map/while/body/eval_jaxpr/jit(cholesky)/cholesky | solution.py:47
  425.8 9.8 %custom-call.87 = f32[1,128,128]{1,2,0:T(8,128)S(1)} custom-call(f32[1,128,128]{2,1,0:T(8,128)S(1)} %get-tuple-element.69), custom_call_target="InvertDiagBlocksLowerTriangular" | custom-call | tf_op jit(solution)/shard_map/while/body/eval_jaxpr/jit(cholesky)/cholesky | solution.py:47
  439.7 11.7 %cholesky.544 = f32[128,128]{1,0:T(8,128)S(1)} custom-call(f32[128,128]{1,0:T(8,128)S(1)} %cholesky.606), custom_call_target="Cholesky" | custom-call | tf_op jit(solution)/shard_map/while/body/eval_jaxpr/jit(cholesky)/cholesky | solution.py:47
  452.2 9.8 %custom-call.88 = f32[1,128,128]{1,2,0:T(8,128)S(1)} custom-call(f32[1,128,128]{2,1,0:T(8,128)S(1)} %get-tuple-element.67), custom_call_target="InvertDiagBlocksLowerTriangular" | custom-call | tf_op jit(solution)/shard_map/while/body/eval_jaxpr/jit(cholesky)/cholesky | solution.py:47
  465.0 11.7 %cholesky.562 = f32[128,128]{1,0:T(8,128)S(1)} custom-call(f32[128,128]{1,0:T(8,128)S(1)} %convolution_subtract_fusion.6), custom_call_target="Cholesky" | custom-call | tf_op jit(solution)/shard_map/while/body/eval_jaxpr/jit(cholesky)/cholesky | solution.py:47
  487.8 4.8 select_select_fusion
  492.7 28.5 %while.1 = (s32[]{:T(128)}, f32[1024,1024]{0,1:T(8,128)}, s32[8,2]{0,1:T(2,128)S(1)}, f32[8,128,128]{2,1,0:T(8,128)}, s32[]{:T(128)}) while((s32[]{:T(128)}, f32[1024,1024]{0,1:T(8,128)}, s32[8,2]{0,1:T(2,128)S(1)}, f32[8,128,128]{2,1,0:T(8,128)}, s32[]{:T(128)}) %tuple.66), condition=%wide.while_cond, body=%wide.while_body.sunk | while | flops 2 | bytes 393829 | solution.py:55
  521.2 79.5 %custom-call.89 = f32[8,128,128]{1,2,0:T(8,128)S(1)} custom-call(f32[8,128,128]{2,1,0:T(8,128)} %get-tuple-element.27), custom_call_target="InvertDiagBlocksLowerTriangular" | custom-call | tf_op jit(solution)/shard_map/while/body/eval_jaxpr/jit(_solve_triangular)/triangular_solve | solution.py:55
  (196 shorter events, 98.9 us)
Async XLA Ops:
  17.9 8.1 %copy-start.4 = (s32[1,48]{1,0:T(1,128)S(1)}, s32[1,48]{1,0:T(1,128)}, u32[]{:S(2)}) copy-start(s32[1,48]{1,0:T(1,128)} %param.4) | copy-start | bytes 580
  17.9 8.3 %copy-start.5 = (s32[1,8]{1,0:T(1,128)S(1)}, s32[1,8]{1,0:T(1,128)}, u32[]{:S(2)}) copy-start(s32[1,8]{1,0:T(1,128)} %param.5) | copy-start | bytes 100
  17.9 101.5 %all-to-all-start = ((bf16[2,64,64,512]{3,1,0,2:T(8,128)(2,1)}), bf16[2,64,64,512]{3,1,0,2:T(8,128)(2,1)}, u32[]{:S(2)}, u32[]{:S(2)}) async-start(bf16[2,64,64,512]{3,1,0,2:T(8,128)(2,1)} %copy.107), calls=%async_computation | async-start | bytes 16777216 | tf_op jit(solution)/shard_map/all_to_all | solution.py:91
  151.6 7.8 %all-to-all-start.1 = ((bf16[2,2,32,512]{3,2,0,1:T(8,128)(2,1)}), bf16[2,2,32,512]{3,2,0,1:T(8,128)(2,1)S(1)}, u32[]{:S(2)}, u32[]{:S(2)}) async-start(bf16[2,2,32,512]{3,2,0,1:T(8,128)(2,1)} %copy.109), calls=%async_computation.1 | async-start | bytes 262144 | tf_op jit(solution)/shard_map/all_to_all | solution.py:97
  155.0 101.7 %all-reduce.3.cloned.1.call-start = ((), (), s32[]{:S(2)}) async-start(), calls=%async_computation.2 | async-start | bytes 2097152 | tf_op jit(solution)/shard_map/psum | solution.py:106
  256.7 2.8 copy-start.2
  258.1 1.3 copy-start.3
  278.6 1.9 copy-start.1
  328.7 2.0 copy-start
Sparse Core Ops, SparseCore 0:
  162.5 94.1 all-reduce.2
where the time goes:
time: 636 us; the launch traced here: 630 us
  other arithmetic  266 us (42%)
  waiting for transfers between devices  192 us (30%)
  local copies, waits for them, and re-layouts  88.4 us (14%)
  matrix products  53.1 us (8%)
  between operations  19.9 us (3%)
  starting transfers between devices  11 us (2%)
    another operation x31, other arithmetic, solve_weights(): factor = jnp.linalg.cholesky(covariance)  168 us
    psum x1, waiting for transfers between devices, on_device(): summed = lax.psum(packed_all, 'rng')  94.3 us
    all_to_all x1, waiting for transfers between devices, on_device(): lax.all_to_all(radar_cube, 'dop', split_axis=2, concat_axis=1, tiled=True)  92.9 us
    another operation x4, other arithmetic, solve_weights(): jax.scipy.linalg.solve_triangular(factor, whitened / lengths[None, :], tr...  84.4 us
    unnamed x29, local copies, waits for them, and re-layouts  30.9 us
    another operation x40, local copies, waits for them, and re-layouts  28.4 us
    another operation x14, matrix products, solve_weights(): factor = jnp.linalg.cholesky(covariance)  26.1 us
  transfers between devices with their start and end apart: 3, of which 3 were waited for; matrix products, arithmetic and copies ran while one was open for 0% of the time, Pallas kernels for 0%

commit v1 on v0

v1 whole, which is shorter than its diff:
```python
import math

import jax
import jax.numpy as jnp
import numpy as np
from jax import lax
from jax.experimental import pallas as pl
from jax.experimental.pallas import tpu as pltpu
from jax.sharding import PartitionSpec as P

NANG = 256
LOAD_EPS = 1e-05
HALF = 64
LANES = 128
SUB = 8
HIGH = lax.Precision.HIGHEST


def doppler_table(bin_count, pulses):
    phase = (np.arange(bin_count)[:, None] * (pulses // bin_count) * np.arange(pulses)[None, :] % pulses) * (
        2.0 * math.pi / pulses
    )
    cosine = jnp.asarray(np.cos(phase), jnp.float32).astype(jnp.bfloat16).astype(jnp.float32)
    sine = jnp.asarray(np.sin(phase), jnp.float32).astype(jnp.bfloat16).astype(jnp.float32)
    upper = jnp.stack([cosine, sine], 1)
    lower = jnp.stack([-sine, cosine], 1)
    return jnp.stack([upper, lower], 0)


def partial_kernel(classes, outs, coef_ref, cube_ref, out_ref):
    local = cube_ref.shape[1]
    folded = []
    for part in range(2):
        for cls in range(classes):
            total = cube_ref[part, cls].astype(jnp.float32)
            for pulse in range(cls + classes, local, classes):
                total = total + cube_ref[part, pulse].astype(jnp.float32)
            folded.append(total)
    for row in range(outs):
        acc = folded[0] * coef_ref[row, 0]
        for col in range(1, 2 * classes):
            acc = acc + folded[col] * coef_ref[row, col]
        out_ref[row] = acc


def partial_spectra(cube, coef, classes):
    _, local, gates, channels = cube.shape
    rows = coef.shape[0]
    step = 16
    width = min(channels, 256)
    return pl.pallas_call(
        lambda *refs: partial_kernel(classes, rows, *refs),
        grid=(gates // step, channels // width),
        in_specs=[
            pl.BlockSpec(memory_space=pltpu.SMEM),
            pl.BlockSpec((2, local, step, width), lambda i, j: (0, 0, i, j)),
        ],
        out_specs=pl.BlockSpec((rows, step, width), lambda i, j: (0, i, j)),
        out_shape=jax.ShapeDtypeStruct((rows, gates, channels), jnp.float32),
        name="partial_spectra",
    )(coef, cube)


def finish_kernel(scale, *refs):
    gates_ref, *parts, spec_ref, pack_ref = refs
    train = gates_ref.shape[1]
    gates = spec_ref.shape[1]
    shift = gates - train
    index = lax.broadcasted_iota(jnp.int32, (1, train), 1)
    same = jnp.where(gates_ref[...] == index, 1.0, 0.0)
    start = jnp.sum(same, axis=1, keepdims=True)
    row = lax.broadcasted_iota(jnp.int32, (train, LANES), 0).astype(jnp.float32)
    early = row < start
    lane = lax.broadcasted_iota(jnp.int32, (train, LANES), 1)
    low = lane < HALF
    for tile in range(spec_ref.shape[2] // LANES):
        cols = slice(tile * LANES, (tile + 1) * LANES)
        picked = []
        for part in range(2):
            total = parts[0][part, :, cols]
            for other in parts[1:]:
                total = total + other[part, :, cols]
            value = (total * scale).astype(jnp.bfloat16)
            spec_ref[part, :, cols] = value
            value = value.astype(jnp.float32)
            picked.append(jnp.where(early, value[:train], value[shift:]))
        real, imag = picked
        first = jnp.where(low, real, pltpu.roll(imag, HALF, 1))
        second = jnp.where(low, pltpu.roll(real, HALF, 1), imag)
        base = 2 * tile * LANES
        pack_ref[:, base : base + LANES] = first.astype(jnp.bfloat16)
        pack_ref[:, base + LANES : base + 2 * LANES] = second.astype(jnp.bfloat16)


def finish_spectra(gate_row, parts, scale):
    _, gates, channels = parts[0].shape
    train = gate_row.shape[1]
    return pl.pallas_call(
        lambda *refs: finish_kernel(scale, *refs),
        out_shape=(
            jax.ShapeDtypeStruct((2, gates, channels), jnp.bfloat16),
            jax.ShapeDtypeStruct((train, 2 * channels), jnp.bfloat16),
        ),
        name="finish_spectra",
    )(gate_row, *parts)


def spread(value, row):
    return jnp.broadcast_to(value[row : row + 1, :], (SUB, LANES))


def lane_spread(value, lane):
    return jnp.broadcast_to(value[:, lane : lane + 1], (SUB, LANES))


def tree_sum(terms):
    terms = list(terms)
    while len(terms) > 1:
        nxt = [terms[i] + terms[i + 1] for i in range(0, len(terms) - 1, 2)]
        if len(terms) % 2:
            nxt.append(terms[-1])
        terms = nxt
    return terms[0]


def invert_rows(real_cols, imag_cols, rows, turned, sub):
    scale = None
    for j in range(SUB):
        recip = 1.0 / spread(real_cols[j], j)
        own = sub == j
        scale = recip if scale is None else jnp.where(own, recip, scale)
        sr = jnp.where(own, 0.0, real_cols[j] * recip)
        si = jnp.where(own, 0.0, imag_cols[j] * recip)
        for l in range(j + 1, SUB):
            ur = spread(real_cols[l], j)
            ui = spread(imag_cols[l], j)
            real_cols[l] = real_cols[l] - (sr * ur - si * ui)
            imag_cols[l] = imag_cols[l] - (sr * ui + si * ur)
        one = spread(rows, j)
        two = spread(turned, j)
        rows = rows - (sr * one + si * two)
        turned = turned - (sr * two - si * one)
    return rows * scale, turned * scale


def invert_block(tiles, lane, sub, sign):
    count = len(tiles)
    for t in range(count):
        k = SUB * t
        in_re = (lane >= k) & (lane < k + SUB)
        in_im = (lane >= HALF + k) & (lane < HALF + k + SUB)
        inside = in_re | in_im
        real_cols = [lane_spread(tiles[t], k + l) for l in range(SUB)]
        imag_cols = [lane_spread(tiles[t], HALF + k + l) for l in range(SUB)]
        unit = jnp.where(in_re & (lane - k == sub), 1.0, 0.0)
        rows = jnp.where(inside, unit, tiles[t])
        turned = pltpu.roll(rows, HALF, 1) * sign
        rows, turned = invert_rows(real_cols, imag_cols, rows, turned, sub)
        ones = [spread(rows, l) for l in range(SUB)]
        twos = [spread(turned, l) for l in range(SUB)]
        fresh = list(tiles)
        fresh[t] = rows
        for i in list(range(t + 1, count)) + list(range(t)):
            terms = []
            for l in range(SUB):
                cr = lane_spread(tiles[i], k + l)
                ci = lane_spread(tiles[i], HALF + k + l)
                terms.append(cr * ones[l] + ci * twos[l])
            fresh[i] = jnp.where(inside, 0.0, tiles[i]) - tree_sum(terms)
        tiles = fresh
    return tiles


def turn(value, sign):
    tiles = value.shape[1] // LANES
    out = [
        pltpu.roll(value[:, t * LANES : (t + 1) * LANES], HALF, 1) * sign[: value.shape[0]]
        for t in range(tiles)
    ]
    return out[0] if tiles == 1 else jnp.concatenate(out, 1)


def exact_dot(a, b):
    return jnp.dot(a, b, precision=HIGH, preferred_element_type=jnp.float32)


def solve_kernel(train_count, beams, gram_ref, steer_ref, spec_ref, out_ref, mat, xs):
    blocks = gram_ref.shape[0] // LANES
    lane = lax.broadcasted_iota(jnp.int32, (SUB, LANES), 1)
    sub = lax.broadcasted_iota(jnp.int32, (SUB, LANES), 0)
    sign = jnp.where(lane < HALF, -1.0, 1.0)
    blane = lax.broadcasted_iota(jnp.int32, (HALF, LANES), 1)
    brow = lax.broadcasted_iota(jnp.int32, (HALF, LANES), 0)
    bsign = jnp.where(blane < HALF, -1.0, 1.0)
    inv = 1.0 / train_count
    diag = blane == brow
    trace = jnp.zeros((HALF, LANES), jnp.float32)
    for i in range(blocks):
        for j in range(blocks):
            top = gram_ref[i * LANES : i * LANES + HALF, j * LANES : (j + 1) * LANES]
            low = gram_ref[i * LANES + HALF : (i + 1) * LANES, j * LANES : (j + 1) * LANES]
            value = (pltpu.roll(low, HALF, 1) - top * bsign) * inv
            mat[i * HALF : (i + 1) * HALF, j * LANES : (j + 1) * LANES] = value
            if i == j:
                trace = trace + jnp.where(diag, value, 0.0)
        mat[i * HALF : (i + 1) * HALF, blocks * LANES :] = steer_ref[i * HALF : (i + 1) * HALF, :]
    load = LOAD_EPS * jnp.sum(trace, keepdims=True) / (blocks * HALF)
    for i in range(blocks):
        at = (slice(i * HALF, (i + 1) * HALF), slice(i * LANES, (i + 1) * LANES))
        mat[at] = mat[at] + jnp.where(diag, load, 0.0)

    norm = jnp.zeros((HALF, LANES), jnp.float32)
    for k in range(blocks):
        rows = slice(k * HALF, (k + 1) * HALF)
        tiles = [
            mat[k * HALF + SUB * t : k * HALF + SUB * (t + 1), k * LANES : (k + 1) * LANES]
            for t in range(HALF // SUB)
        ]
        inverse = jnp.concatenate(invert_block(tiles, lane, sub, sign), 0)
        right = mat[rows, (k + 1) * LANES :]
        upper = exact_dot(inverse, jnp.concatenate([right, turn(right, bsign)], 0))
        norm = norm + right[:, -LANES:] * upper[:, -LANES:]
        mat[rows, (k + 1) * LANES :] = upper
        if k + 1 < blocks:
            below = slice((k + 1) * HALF, blocks * HALF)
            both = jnp.concatenate([upper, turn(upper, bsign)], 0)
            mat[below, (k + 1) * LANES :] = mat[below, (k + 1) * LANES :] - exact_dot(
                mat[below, k * LANES : (k + 1) * LANES], both
            )
    total = jnp.sum(norm, axis=0, keepdims=True)
    total = total + pltpu.roll(jnp.broadcast_to(total, (SUB, LANES)), HALF, 1)[:1]
    low8 = (blane[:1] % HALF) < beams
    factor = jnp.where(low8, lax.rsqrt(jnp.where(low8, total, 1.0)), 0.0)
    for k in reversed(range(blocks)):
        rows = slice(k * HALF, (k + 1) * HALF)
        value = mat[rows, blocks * LANES :]
        if k + 1 < blocks:
            value = value - exact_dot(
                mat[rows, (k + 1) * LANES : blocks * LANES], xs[(k + 1) * LANES : blocks * LANES, :]
            )
        xs[k * LANES : k * LANES + HALF, :] = value
        xs[k * LANES + HALF : (k + 1) * LANES, :] = turn(value, bsign)
    weights = jnp.concatenate(
        [(xs[k * LANES : k * LANES + HALF, :] * factor).astype(jnp.bfloat16) for k in range(blocks)], 0
    )
    contract = (((0,), (1,)), ((), ()))
    real = lax.dot_general(weights, spec_ref[0], contract, preferred_element_type=jnp.float32)
    imag = lax.dot_general(weights, spec_ref[1], contract, preferred_element_type=jnp.float32)
    out_ref[0] = real[:beams] + imag[HALF : HALF + beams]
    out_ref[1] = real[HALF : HALF + beams] - imag[:beams]


def solve_and_filter(gram, steer, spectrum, train_count, beams):
    channels = gram.shape[0] // 2
    gates = spectrum.shape[1]
    return pl.pallas_call(
        lambda *refs: solve_kernel(train_count, beams, *refs),
        out_shape=jax.ShapeDtypeStruct((2, beams, gates), jnp.float32),
        scratch_shapes=[
            pltpu.VMEM((channels, 2 * channels + LANES), jnp.float32),
            pltpu.VMEM((2 * channels, LANES), jnp.float32),
        ],
        name="solve_and_filter",
    )(gram, steer, spectrum)


def packed_steering(look_row, channels, angle_count):
    beams = look_row.shape[0]
    slope = 2 * look_row + 1 - angle_count
    half = jnp.pad(slope, (0, HALF - beams))
    lane = jnp.arange(LANES, dtype=jnp.int32)
    channel = jnp.arange(channels, dtype=jnp.int32)
    index = channel[:, None] * jnp.concatenate([half, half])[None, :]
    index = (index - jnp.where(lane >= HALF, angle_count // 2, 0)[None, :]) % (2 * angle_count)
    value = jnp.cos(index.astype(jnp.float32) * (math.pi / angle_count))
    return jnp.where((lane % HALF < beams)[None, :], value, 0.0)


def on_device(radar_cube, train_gates, look_angles):
    dop = lax.axis_size("dop")
    rng = lax.axis_size("rng")
    me = lax.axis_index("dop")
    local = radar_cube.shape[1]
    pulses = local * dop
    channels = radar_cube.shape[3]
    bins = dop * train_gates.shape[0]
    beams = look_angles.shape[1]
    classes = bins if local % bins == 0 else local
    table = doppler_table(bins, pulses)
    table = lax.dynamic_slice_in_dim(table, me * local, classes, axis=3)
    table = jnp.roll(table, -me, axis=1)
    coef = jnp.transpose(table, (1, 0, 2, 3)).reshape(2 * bins, 2 * classes)
    parts = partial_spectra(radar_cube, coef, classes)
    parts = parts.reshape(bins, 2, *parts.shape[1:])
    mine = [parts[0]]
    for hop in range(1, dop):
        pairs = [(d, (d + hop) % dop) for d in range(dop)]
        mine.append(lax.ppermute(parts[hop], "dop", pairs))
    spectrum, packed = finish_spectra(train_gates, mine, 1.0 / math.sqrt(pulses))
    gathered = lax.all_gather(packed, "rng", axis=0, tiled=True)
    gram = lax.dot_general(
        gathered, gathered, (((0,), (0,)), ((), ())), preferred_element_type=jnp.float32
    )
    steer = packed_steering(look_angles[0], channels, NANG)
    out = solve_and_filter(gram, steer, spectrum, train_gates.shape[1] * rng, beams)
    return out[:, None]


def solution(mesh):
    placed = (P(None, "dop", "rng", None), P("dop", "rng"), P("dop", None))
    return jax.shard_map(
        on_device,
        mesh=mesh,
        in_specs=placed,
        out_specs=P(None, "dop", None, "rng"),
        check_vma=False,
    )
```

time: 636 us -> 116 us (0.18)
  other arithmetic: 266 us -> 1.78 us
  waiting for transfers between devices: 192 us -> 45.7 us
  local copies, waits for them, and re-layouts: 88.4 us -> 3.91 us
  matrix products: 53.1 us -> 5.65 us
  Pallas kernels: 0 us -> 42.3 us
  starting transfers between devices: 11 us -> 3 us
  between operations: 19.9 us -> 13.4 us
    another operation x36 -> x0, other arithmetic: 253 us -> none  [the longest x31 168 us: solve_weights(): factor = jnp.linalg.cholesky(covariance)]
    all_to_all x2 -> x0, waiting for transfers between devices: 97.3 us -> none  [the longest x1 92.9 us: on_device(): lax.all_to_all(radar_cube, 'dop', split_axis=2, concat_axis=1, tiled=True)]
    psum x1 -> x0, waiting for transfers between devices: 94.3 us -> none  [on_device(): summed = lax.psum(packed_all, 'rng')]
    another operation x44 -> x0, matrix products: 46.6 us -> none  [the longest x14 26.1 us: solve_weights(): factor = jnp.linalg.cholesky(covariance)]
    pallas_call x0 -> x3, Pallas kernels: none -> 42.3 us  [the longest x1 33.1 us: solve_and_filter(): pl.pallas_call(lambda *refs: solve_kernel(train_count, beams, *refs), out...]
    all_gather x0 -> x1, waiting for transfers between devices: none -> 39.4 us  [on_device(): gathered = lax.all_gather(packed, 'rng', axis=0, tiled=True)]
    another operation x69 -> x0, local copies, waits for them, and re-layouts: 34.2 us -> none
    unnamed x29 -> x4, local copies, waits for them, and re-layouts: 30.9 us -> 0.7 us
  transfers between devices with their start and end apart: 3 -> 2, of which waited for: 3 -> 2; matrix products, arithmetic and copies ran while one was open for 0% -> 2% of each run, Pallas kernels for 0% -> 0%
where the time goes in v1:
time: 116 us
  waiting for transfers between devices  45.7 us (39%)
  Pallas kernels  42.3 us (36%)
  between operations  13.4 us (12%)
  matrix products  5.65 us (5%)
  local copies, waits for them, and re-layouts  3.91 us (3%)
  starting transfers between devices  3 us (3%)
  other arithmetic  1.78 us (2%)
    all_gather x1, waiting for transfers between devices, on_device(): gathered = lax.all_gather(packed, 'rng', axis=0, tiled=True)  39.4 us
    pallas_call x1, Pallas kernels, solve_and_filter(): pl.pallas_call(lambda *refs: solve_kernel(train_count, beams, *refs), out...  33.1 us
    pallas_call x1, Pallas kernels, partial_spectra(): pl.pallas_call(lambda *refs: partial_kernel(classes, rows, *refs), grid=(...  7.36 us
    ppermute x1, waiting for transfers between devices, on_device(): mine.append(lax.ppermute(parts[hop], 'dop', pairs))  6.3 us
    dot_general x1, matrix products, on_device(): lax.dot_general(gathered, gathered, (((0,), (0,)), ((), ())), preferred_e...  5.65 us
    ppermute x1, starting transfers between devices, on_device(): mine.append(lax.ppermute(parts[hop], 'dop', pairs))  3 us
  transfers between devices with their start and end apart: 2, of which 2 were waited for; matrix products, arithmetic and copies ran while one was open for 2% of the time, Pallas kernels for 0%

profile of v1, /device:TPU:0, one launch (start us, length us, event | category | flops | bytes accessed | tf_op | source)
XLA Modules:
  0.0 115.8 jit_solution(3609959071457768618)
XLA Ops:
  6.5 0.0 all-gather.2.cloned.1.call-start
  6.5 0.8 constant_dynamic-slice_fusion
  7.3 0.7 reshape.28.refs_0_
  8.0 7.4 %partial_spectra.1 = f32[4,64,512]{2,1,0:T(8,128)} custom-call(f32[4,4]{1,0:T(4,128)} %reshape.28.refs_0_, bf16[2,64,64,512]{3,2,1,0:T(8,128)(2,1)} %refs_1_.1), custom_call_target="tpu_custom_call" | custom-call | tf_op jit(solution)/shard_map/partial_spectra/pallas_call | solution.py:51
  15.3 0.0 copy-start.1
  15.3 1.8 %fusion.8 = (f32[2,64,512]{2,1,0:T(8,128)S(1)}, f32[2,64,512]{2,1,0:T(8,128)}) fusion(f32[4,64,512]{2,1,0:T(8,128)} %partial_spectra.1), kind=kLoop, calls=%fused_computation.18 | loop fusion | bytes 1048576 | tf_op jit(solution)/shard_map/slice | solution.py:298
  17.1 3.0 %collective-permute-start = (f32[2,64,512]{2,1,0:T(8,128)S(1)}, f32[2,64,512]{2,1,0:T(8,128)S(1)}, u32[]{:S(2)}, u32[]{:S(2)}) collective-permute-start(f32[2,64,512]{2,1,0:T(8,128)S(1)} %get-tuple-element.9), channel_id=1, source_target_pairs={{0,16},{16,0},{1,17},{17,1},{2,18},{18,2},{3,19},{19,3},{4,20},{20... | collective-permute-start | bytes 786440 | tf_op jit(solution)/shard_map/ppermute | solution.py:298
  20.1 6.3 %collective-permute-done.refs_2_ = f32[2,64,512]{2,1,0:T(8,128)S(1)} collective-permute-done((f32[2,64,512]{2,1,0:T(8,128)S(1)}, f32[2,64,512]{2,1,0:T(8,128)S(1)}, u32[]{:S(2)}, u32[]{:S(2)}) %collective-permute-start) | collective-permute-done | bytes 262176 | tf_op jit(solution)/shard_map/ppermute | solution.py:298
  26.4 0.0 copy-start
  26.4 0.7 copy-done
  27.1 1.9 %finish_spectra.1 = (bf16[2,64,512]{2,1,0:T(8,128)(2,1)}, bf16[48,1024]{1,0:T(8,128)(2,1)}) custom-call(s32[1,48]{1,0:T(1,128)} %refs_0_.1, f32[2,64,512]{2,1,0:T(8,128)} %get-tuple-element.10.refs_1_, f32[2,64,512]{2,1,0:T(8,128)} %copy-done), custom_call_target="tpu_custom_call" | custom-call | tf_op jit(solution)/shard_map/finish_spectra/pallas_call | solution.py:98
  29.0 0.0 all-gather.2.cloned.1.call-update
  29.0 0.0 copy-done.1
  29.1 0.1 compare_select_fusion
  29.2 1.7 %fusion.4.refs_1_ = f32[512,128]{1,0:T(8,128)} fusion(s32[128]{0:T(128)S(1)} %get-tuple-element.11, s32[128]{0:T(128)S(1)} %get-tuple-element.12, pred[128]{0:T(512)(128)(4,1)S(1)} %fusion.7), kind=kLoop, calls=%fused_computation.7 | loop fusion | flops 1048576 | bytes 263296 | tf_op jit(solution)/shard_map/jit(_where)/select_n | solution.py:276
  30.8 39.4 %all-gather.2.cloned.1.call-done = bf16[768,1024]{1,0:T(8,128)(2,1)} async-done(((bf16[48,1024]{1,0:T(8,128)(2,1)}), bf16[768,1024]{1,0:T(8,128)(2,1)}) %all-gather.2.cloned.1.call-update) | async-done | bytes 1572880 | tf_op jit(solution)/shard_map/all_gather | solution.py:300
  70.2 5.7 %fusion.9.refs_0_ = f32[1024,1024]{1,0:T(8,128)} fusion(bf16[768,1024]{1,0:T(8,128)(2,1)} %all-gather.2.cloned.1.call-done), kind=kOutput, calls=%fused_computation.19 | convolution fusion | flops 1610612736 | bytes 5767168 | tf_op jit(solution)/shard_map/dot_general | solution.py:301
  75.9 33.1 %solve_and_filter.1 = f32[2,8,64]{2,1,0:T(8,128)} custom-call(f32[1024,1024]{1,0:T(8,128)} %fusion.9.refs_0_, f32[512,128]{1,0:T(8,128)} %fusion.4.refs_1_, bf16[2,64,512]{2,1,0:T(8,128)(2,1)} %get-tuple-element.8.refs_2_), custom_call_target="tpu_custom_call" | custom-call | tf_op jit(solution)/shard_map/solve_and_filter/pallas_call | solution.py:256
  (4 shorter events, 0.0 us)
Async XLA Ops:
  6.5 63.7 %all-gather.2.cloned.1.call-start = ((), (), s32[]{:S(2)}) async-start(), calls=%async_computation | async-start | bytes 1671168 | tf_op jit(solution)/shard_map/all_gather | solution.py:300
  15.3 13.7 %copy-start.1 = (s32[1,8]{1,0:T(1,128)S(1)}, s32[1,8]{1,0:T(1,128)}, u32[]{:S(2)}) copy-start(s32[1,8]{1,0:T(1,128)} %param.7) | copy-start | bytes 100
  17.1 9.3 %collective-permute-start = (f32[2,64,512]{2,1,0:T(8,128)S(1)}, f32[2,64,512]{2,1,0:T(8,128)S(1)}, u32[]{:S(2)}, u32[]{:S(2)}) collective-permute-start(f32[2,64,512]{2,1,0:T(8,128)S(1)} %get-tuple-element.9), channel_id=1, source_target_pairs={{0,16},{16,0},{1,17},{17,1},{2,18},{18,2},{3,19},{19,3},{4,20},{20... | collective-permute-start | bytes 786440 | tf_op jit(solution)/shard_map/ppermute | solution.py:298
  26.4 0.7 copy-start
Sparse Core Ops, SparseCore 0:
  29.1 41.0 all-gather.1

commit v2 on v1

--- a/solution.py
+++ b/solution.py
@@ -20,45 +20,59 @@
     phase = (np.arange(bin_count)[:, None] * (pulses // bin_count) * np.arange(pulses)[None, :] % pulses) * (
         2.0 * math.pi / pulses
     )
-    cosine = jnp.asarray(np.cos(phase), jnp.float32).astype(jnp.bfloat16).astype(jnp.float32)
-    sine = jnp.asarray(np.sin(phase), jnp.float32).astype(jnp.bfloat16).astype(jnp.float32)
-    upper = jnp.stack([cosine, sine], 1)
-    lower = jnp.stack([-sine, cosine], 1)
-    return jnp.stack([upper, lower], 0)
-
-
-def partial_kernel(classes, outs, coef_ref, cube_ref, out_ref):
-    local = cube_ref.shape[1]
-    folded = []
-    for part in range(2):
-        for cls in range(classes):
-            total = cube_ref[part, cls].astype(jnp.float32)
-            for pulse in range(cls + classes, local, classes):
-                total = total + cube_ref[part, pulse].astype(jnp.float32)
-            folded.append(total)
-    for row in range(outs):
-        acc = folded[0] * coef_ref[row, 0]
-        for col in range(1, 2 * classes):
-            acc = acc + folded[col] * coef_ref[row, col]
-        out_ref[row] = acc
-
-
-def partial_spectra(cube, coef, classes):
+    cosine = np.cos(phase).astype(np.float32).astype(jnp.bfloat16).astype(np.float32)
+    sine = np.sin(phase).astype(np.float32).astype(jnp.bfloat16).astype(np.float32)
+    upper = np.stack([cosine, sine], 1)
+    lower = np.stack([-sine, cosine], 1)
+    return np.stack([upper, lower], 0)
+
+
+def pick(values, index):
+    if all(v == values[0] for v in values):
+        return float(values[0])
+    out = jnp.float32(values[0])
+    for i, v in enumerate(values[1:], 1):
+        out = jnp.where(index == i, jnp.float32(v), out)
+    return out
+
+
+def partial_kernel(classes, dop, table, *refs):
+    cube_ref, *out_refs = refs
+    me = lax.axis_index("dop")
+    local, _, width = cube_ref.shape[1:]
+    for base in range(0, width, LANES):
+        cols = slice(base, base + LANES)
+        folded = []
+        for part in range(2):
+            for cls in range(classes):
+                total = cube_ref[part, cls, :, cols].astype(jnp.float32)
+                for pulse in range(cls + classes, local, classes):
+                    total = total + cube_ref[part, pulse, :, cols].astype(jnp.float32)
+                folded.append(total)
+        for slot, out_ref in enumerate(out_refs):
+            for row in range(2):
+                acc = None
+                for part in range(2):
+                    for cls in range(classes):
+                        options = [
+                            table[row, (d + slot) % dop, part, d * local + cls] for d in range(dop)
+                        ]
+                        term = folded[part * classes + cls] * pick(options, me)
+                        acc = term if acc is None else acc + term
+                out_ref[row, :, cols] = acc
+
+
+def partial_spectra(cube, table, classes, dop):
     _, local, gates, channels = cube.shape
-    rows = coef.shape[0]
     step = 16
-    width = min(channels, 256)
     return pl.pallas_call(
-        lambda *refs: partial_kernel(classes, rows, *refs),
-        grid=(gates // step, channels // width),
-        in_specs=[
-            pl.BlockSpec(memory_space=pltpu.SMEM),
-            pl.BlockSpec((2, local, step, width), lambda i, j: (0, 0, i, j)),
-        ],
-        out_specs=pl.BlockSpec((rows, step, width), lambda i, j: (0, i, j)),
-        out_shape=jax.ShapeDtypeStruct((rows, gates, channels), jnp.float32),
+        lambda *refs: partial_kernel(classes, dop, table, *refs),
+        grid=(gates // step,),
+        in_specs=[pl.BlockSpec((2, local, step, channels), lambda i: (0, 0, i, 0))],
+        out_specs=[pl.BlockSpec((2, step, channels), lambda i: (0, i, 0))] * dop,
+        out_shape=[jax.ShapeDtypeStruct((2, gates, channels), jnp.float32)] * dop,
         name="partial_spectra",
-    )(coef, cube)
+    )(cube)
 
 
 def finish_kernel(scale, *refs):
@@ -276,31 +290,46 @@
     return jnp.where((lane % HALF < beams)[None, :], value, 0.0)
 
 
+def shift_pairs(count, stride, extent, hop):
+    pairs = []
+    for i in range(count):
+        digit = i // stride % extent
+        pairs.append((i, i + ((digit + hop) % extent - digit) * stride))
+    return pairs
+
+
+def gather_rows(rows, count):
+    if count % 4:
+        return (lax.all_gather(rows, "rng", axis=0, tiled=True),)
+    outer = count // 4
+    pieces = [rows]
+    for hop in range(1, outer):
+        pieces.append(lax.ppermute(rows, "rng", shift_pairs(count, 4, outer, hop)))
+    across = [lax.ppermute(piece, "rng", shift_pairs(count, 2, 2, 1)) for piece in pieces]
+    side = jnp.concatenate(pieces + across, 0)
+    return side, lax.ppermute(side, "rng", shift_pairs(count, 1, 2, 1))
+
+
 def on_device(radar_cube, train_gates, look_angles):
     dop = lax.axis_size("dop")
     rng = lax.axis_size("rng")
-    me = lax.axis_index("dop")
     local = radar_cube.shape[1]
     pulses = local * dop
     channels = radar_cube.shape[3]
-    bins = dop * train_gates.shape[0]
     beams = look_angles.shape[1]
-    classes = bins if local % bins == 0 else local
-    table = doppler_table(bins, pulses)
-    table = lax.dynamic_slice_in_dim(table, me * local, classes, axis=3)
-    table = jnp.roll(table, -me, axis=1)
-    coef = jnp.transpose(table, (1, 0, 2, 3)).reshape(2 * bins, 2 * classes)
-    parts = partial_spectra(radar_cube, coef, classes)
-    parts = parts.reshape(bins, 2, *parts.shape[1:])
+    classes = dop if local % dop == 0 else local
+    parts = partial_spectra(radar_cube, doppler_table(dop, pulses), classes, dop)
     mine = [parts[0]]
     for hop in range(1, dop):
         pairs = [(d, (d + hop) % dop) for d in range(dop)]
         mine.append(lax.ppermute(parts[hop], "dop", pairs))
     spectrum, packed = finish_spectra(train_gates, mine, 1.0 / math.sqrt(pulses))
-    gathered = lax.all_gather(packed, "rng", axis=0, tiled=True)
-    gram = lax.dot_general(
-        gathered, gathered, (((0,), (0,)), ((), ())), preferred_element_type=jnp.float32
-    )
+    gram = None
+    for side in gather_rows(packed, rng):
+        term = lax.dot_general(
+            side, side, (((0,), (0,)), ((), ())), preferred_element_type=jnp.float32
+        )
+        gram = term if gram is None else gram + term
     steer = packed_steering(look_angles[0], channels, NANG)
     out = solve_and_filter(gram, steer, spectrum, train_gates.shape[1] * rng, beams)
     return out[:, None]

time: 116 us -> 74.9 us (0.65)
  waiting for transfers between devices: 45.7 us -> 12.5 us
  between operations: 13.4 us -> 0.08 us
  starting transfers between devices: 3 us -> 13.7 us
  local copies, waits for them, and re-layouts: 3.91 us -> 1.69 us
  Pallas kernels: 42.3 us -> 40.4 us
    all_gather x1 -> x0, waiting for transfers between devices: 39.4 us -> none  [on_device(): gathered = lax.all_gather(packed, 'rng', axis=0, tiled=True)]
    ppermute x0 -> x8, starting transfers between devices: none -> 10.7 us  [the longest x3 5.74 us: gather_rows(): pieces.append(lax.ppermute(rows, 'rng', shift_pairs(count, 4, outer, hop)))]
    ppermute x0 -> x8, waiting for transfers between devices: none -> 5.94 us  [the longest x4 4.45 us: gather_rows(): lax.ppermute(piece, 'rng', shift_pairs(count, 2, 2, 1))]
    pallas_call x1, Pallas kernels: 7.36 us -> 5.5 us  [partial_spectra(): pl.pallas_call(lambda *refs: partial_kernel(classes, dop, table, *refs),...]
    slice x1 -> x0, local copies, waits for them, and re-layouts: 1.79 us -> none  [on_device(): mine.append(lax.ppermute(parts[hop], 'dop', pairs))]
    dot_general x1 -> x2, matrix products: 5.65 us -> 4.57 us  [on_device(): lax.dot_general(side, side, (((0,), (0,)), ((), ())), preferred_element_t...]
  transfers between devices with their start and end apart: 2 -> 9, of which waited for: 2 -> 6; matrix products, arithmetic and copies ran while one was open for 2% -> 4% of each run, Pallas kernels for 0% -> 0%
where the time goes in v2:
time: 74.9 us; the launch traced here: 74.7 us
  Pallas kernels  40.4 us (54%)
  starting transfers between devices  13.7 us (18%)
  waiting for transfers between devices  12.5 us (17%)
  matrix products  4.57 us (6%)
  other arithmetic  1.77 us (2%)
  local copies, waits for them, and re-layouts  1.69 us (2%)
    pallas_call x1, Pallas kernels, solve_and_filter(): pl.pallas_call(lambda *refs: solve_kernel(train_count, beams, *refs), out...  33.1 us
    ppermute x1, waiting for transfers between devices, on_device(): mine.append(lax.ppermute(parts[hop], 'dop', pairs))  6.51 us
    ppermute x3, starting transfers between devices, gather_rows(): pieces.append(lax.ppermute(rows, 'rng', shift_pairs(count, 4, outer, hop)))  5.74 us
    pallas_call x1, Pallas kernels, partial_spectra(): pl.pallas_call(lambda *refs: partial_kernel(classes, dop, table, *refs),...  5.5 us
    ppermute x4, starting transfers between devices, gather_rows(): lax.ppermute(piece, 'rng', shift_pairs(count, 2, 2, 1))  4.86 us
    dot_general x2, matrix products, on_device(): lax.dot_general(side, side, (((0,), (0,)), ((), ())), preferred_element_t...  4.57 us
    ppermute x4, waiting for transfers between devices, gather_rows(): lax.ppermute(piece, 'rng', shift_pairs(count, 2, 2, 1))  4.45 us
    ppermute x1, starting transfers between devices, on_device(): mine.append(lax.ppermute(parts[hop], 'dop', pairs))  3 us
  transfers between devices with their start and end apart: 9, of which 6 were waited for; matrix products, arithmetic and copies ran while one was open for 4% of the time, Pallas kernels for 0%

profile of v2, /device:TPU:0, one launch (start us, length us, event | category | flops | bytes accessed | tf_op | source)
XLA Modules:
  0.0 74.7 jit_solution(13052535066460946025)
XLA Ops:
  0.0 0.0 copy-start.1
  0.0 5.5 %partial_spectra.1 = (f32[2,64,512]{2,1,0:T(8,128)}, f32[2,64,512]{2,1,0:T(8,128)}) custom-call(bf16[2,64,64,512]{3,2,1,0:T(8,128)(2,1)} %refs_0_.2), custom_call_target="tpu_custom_call" | custom-call | tf_op jit(solution)/shard_map/partial_spectra/pallas_call | solution.py:68
  5.5 3.0 %collective-permute-start = (f32[2,64,512]{2,1,0:T(8,128)}, f32[2,64,512]{2,1,0:T(8,128)S(1)}, u32[]{:S(2)}, u32[]{:S(2)}) collective-permute-start(f32[2,64,512]{2,1,0:T(8,128)} %get-tuple-element.10), channel_id=1, source_target_pairs={{0,16},{16,0},{1,17},{17,1},{2,18},{18,2},{3,19},{19,3},{4,20},{20... | collective-permute-start | bytes 786440 | tf_op jit(solution)/shard_map/ppermute | solution.py:325
  8.5 6.5 %collective-permute-done.refs_2_ = f32[2,64,512]{2,1,0:T(8,128)S(1)} collective-permute-done((f32[2,64,512]{2,1,0:T(8,128)}, f32[2,64,512]{2,1,0:T(8,128)S(1)}, u32[]{:S(2)}, u32[]{:S(2)}) %collective-permute-start) | collective-permute-done | bytes 262176 | tf_op jit(solution)/shard_map/ppermute | solution.py:325
  15.0 0.0 copy-start
  15.0 0.7 copy-done
  15.7 1.9 %finish_spectra.1 = (bf16[2,64,512]{2,1,0:T(8,128)(2,1)}, bf16[48,1024]{1,0:T(8,128)(2,1)}) custom-call(s32[1,48]{1,0:T(1,128)} %refs_0_.3, f32[2,64,512]{2,1,0:T(8,128)} %get-tuple-element.9.refs_1_, f32[2,64,512]{2,1,0:T(8,128)} %copy-done), custom_call_target="tpu_custom_call" | custom-call | tf_op jit(solution)/shard_map/finish_spectra/pallas_call | solution.py:112
  17.6 1.8 %collective-permute-start.1 = (bf16[48,1024]{1,0:T(8,128)(2,1)}, bf16[48,1024]{1,0:T(8,128)(2,1)S(1)}, u32[]{:S(2)}, u32[]{:S(2)}) collective-permute-start(bf16[48,1024]{1,0:T(8,128)(2,1)} %get-tuple-element.11), channel_id=1, source_target_pairs={{0,4},{1,5},{2,6},{3,7},{4,8},{5,9},{6,10},{7,11},{8,12},{9,13},{1... | collective-permute-start | bytes 294920 | tf_op jit(solution)/shard_map/ppermute | solution.py:307
  19.4 2.6 %collective-permute-start.2 = (bf16[48,1024]{1,0:T(8,128)(2,1)}, bf16[48,1024]{1,0:T(8,128)(2,1)S(1)}, u32[]{:S(2)}, u32[]{:S(2)}) collective-permute-start(bf16[48,1024]{1,0:T(8,128)(2,1)} %get-tuple-element.11), channel_id=1, source_target_pairs={{0,8},{1,9},{2,10},{3,11},{4,12},{5,13},{6,14},{7,15},{8,0},{9,1},... | collective-permute-start | bytes 294920 | tf_op jit(solution)/shard_map/ppermute | solution.py:307
  22.0 1.3 %collective-permute-start.3 = (bf16[48,1024]{1,0:T(8,128)(2,1)}, bf16[48,1024]{1,0:T(8,128)(2,1)S(1)}, u32[]{:S(2)}, u32[]{:S(2)}) collective-permute-start(bf16[48,1024]{1,0:T(8,128)(2,1)} %get-tuple-element.11), channel_id=1, source_target_pairs={{0,12},{1,13},{2,14},{3,15},{4,0},{5,1},{6,2},{7,3},{8,4},{9,5},{1... | collective-permute-start | bytes 294920 | tf_op jit(solution)/shard_map/ppermute | solution.py:307
  23.3 1.5 %collective-permute-start.4 = (bf16[48,1024]{1,0:T(8,128)(2,1)}, bf16[48,1024]{1,0:T(8,128)(2,1)S(1)}, u32[]{:S(2)}, u32[]{:S(2)}) collective-permute-start(bf16[48,1024]{1,0:T(8,128)(2,1)} %get-tuple-element.11), channel_id=1, source_target_pairs={{0,2},{1,3},{2,0},{3,1},{4,6},{5,7},{6,4},{7,5},{8,10},{9,11},{10,... | collective-permute-start | bytes 294920 | tf_op jit(solution)/shard_map/ppermute | solution.py:308
  24.8 0.9 %constant_dynamic-update-slice_fusion.7 = bf16[384,1024]{1,0:T(8,128)(2,1)S(1)} fusion(bf16[48,1024]{1,0:T(8,128)(2,1)} %get-tuple-element.11), kind=kLoop, calls=%fused_computation.16 | loop fusion | bytes 196608
  25.7 0.0 collective-permute-done.1
  25.7 1.3 %collective-permute-start.5 = (bf16[48,1024]{1,0:T(8,128)(2,1)S(1)}, bf16[48,1024]{1,0:T(8,128)(2,1)S(1)}, u32[]{:S(2)}, u32[]{:S(2)}) collective-permute-start(bf16[48,1024]{1,0:T(8,128)(2,1)S(1)} %collective-permute-done.1), channel_id=1, source_target_pairs={{0,2},{1,3},{2,0},{3,1},{4,6},{5,7},{6,4},{7,5},{8,10},{9,11},{10,... | collective-permute-start | bytes 294920 | tf_op jit(solution)/shard_map/ppermute | solution.py:308
  27.0 1.0 %collective-permute-done.2 = bf16[48,1024]{1,0:T(8,128)(2,1)S(1)} collective-permute-done((bf16[48,1024]{1,0:T(8,128)(2,1)}, bf16[48,1024]{1,0:T(8,128)(2,1)S(1)}, u32[]{:S(2)}, u32[]{:S(2)}) %collective-permute-start.2) | collective-permute-done | bytes 98336 | tf_op jit(solution)/shard_map/ppermute | solution.py:307
  28.1 1.5 %collective-permute-start.6 = (bf16[48,1024]{1,0:T(8,128)(2,1)S(1)}, bf16[48,1024]{1,0:T(8,128)(2,1)S(1)}, u32[]{:S(2)}, u32[]{:S(2)}) collective-permute-start(bf16[48,1024]{1,0:T(8,128)(2,1)S(1)} %collective-permute-done.2), channel_id=1, source_target_pairs={{0,2},{1,3},{2,0},{3,1},{4,6},{5,7},{6,4},{7,5},{8,10},{9,11},{10,... | collective-permute-start | bytes 294920 | tf_op jit(solution)/shard_map/ppermute | solution.py:308
  29.6 0.0 collective-permute-done.3
  29.6 0.6 collective-permute-start.7
  30.2 0.0 collective-permute-done.4
  30.2 0.5 collective-permute-done.5
  30.7 2.9 %collective-permute-done.6 = bf16[48,1024]{1,0:T(8,128)(2,1)S(1)} collective-permute-done((bf16[48,1024]{1,0:T(8,128)(2,1)S(1)}, bf16[48,1024]{1,0:T(8,128)(2,1)S(1)}, u32[]{:S(2)}, u32[]{:S(2)}) %collective-permute-start.6) | collective-permute-done | bytes 98336 | tf_op jit(solution)/shard_map/ppermute | solution.py:308
  33.6 1.0 %collective-permute-done.7 = bf16[48,1024]{1,0:T(8,128)(2,1)S(1)} collective-permute-done((bf16[48,1024]{1,0:T(8,128)(2,1)S(1)}, bf16[48,1024]{1,0:T(8,128)(2,1)S(1)}, u32[]{:S(2)}, u32[]{:S(2)}) %collective-permute-start.7) | collective-permute-done | bytes 98336 | tf_op jit(solution)/shard_map/ppermute | solution.py:308
  34.7 0.1 collective-permute-start.8
  34.8 0.0 copy-done.1
  34.8 0.1 compare_select_fusion
  34.9 1.7 %fusion.4.refs_1_ = f32[512,128]{1,0:T(8,128)} fusion(s32[128]{0:T(128)S(1)} %get-tuple-element.13, s32[128]{0:T(128)S(1)} %get-tuple-element.14, pred[128]{0:T(512)(128)(4,1)S(1)} %fusion.5), kind=kLoop, calls=%fused_computation.8 | loop fusion | flops 1048576 | bytes 263296 | tf_op jit(solution)/shard_map/jit(_where)/select_n | solution.py:290
  36.6 0.5 collective-permute-done.8
  37.0 1.3 %fusion.6 = f32[1024,1024]{1,0:T(8,128)S(1)} fusion(bf16[384,1024]{1,0:T(8,128)(2,1)S(1)} %collective-permute-done.8), kind=kOutput, calls=%fused_computation.22 | convolution fusion | flops 805306368 | bytes 4980736 | tf_op jit(solution)/shard_map/dot_general | solution.py:329
  38.3 3.3 %convolution_add_fusion.refs_0_ = f32[1024,1024]{1,0:T(8,128)} fusion(f32[1024,1024]{1,0:T(8,128)S(1)} %fusion.6, bf16[384,1024]{1,0:T(8,128)(2,1)S(1)} %constant_dynamic-update-slice_fusion), kind=kOutput, calls=%fused_computation | convolution fusion | flops 806354944 | bytes 9175040 | tf_op jit(solution)/shard_map/dot_general | solution.py:329
  41.6 33.1 %solve_and_filter.1 = f32[2,8,64]{2,1,0:T(8,128)} custom-call(f32[1024,1024]{1,0:T(8,128)} %convolution_add_fusion.refs_0_, f32[512,128]{1,0:T(8,128)} %fusion.4.refs_1_, bf16[2,64,512]{2,1,0:T(8,128)(2,1)} %get-tuple-element.12.refs_2_), custom_call_target="tpu_custom_call" | custom-call | tf_op jit(solution)/shard_map/solve_and_filter/pallas_call | solution.py:270
  (10 shorter events, 0.1 us)
Async XLA Ops:
  0.0 34.8 %copy-start.1 = (s32[1,8]{1,0:T(1,128)S(1)}, s32[1,8]{1,0:T(1,128)}, u32[]{:S(2)}) copy-start(s32[1,8]{1,0:T(1,128)} %param.5) | copy-start | bytes 100
  5.5 9.5 %collective-permute-start = (f32[2,64,512]{2,1,0:T(8,128)}, f32[2,64,512]{2,1,0:T(8,128)S(1)}, u32[]{:S(2)}, u32[]{:S(2)}) collective-permute-start(f32[2,64,512]{2,1,0:T(8,128)} %get-tuple-element.10), channel_id=1, source_target_pairs={{0,16},{16,0},{1,17},{17,1},{2,18},{18,2},{3,19},{19,3},{4,20},{20... | collective-permute-start | bytes 786440 | tf_op jit(solution)/shard_map/ppermute | solution.py:325
  15.0 0.7 copy-start
  17.6 8.2 %collective-permute-start.1 = (bf16[48,1024]{1,0:T(8,128)(2,1)}, bf16[48,1024]{1,0:T(8,128)(2,1)S(1)}, u32[]{:S(2)}, u32[]{:S(2)}) collective-permute-start(bf16[48,1024]{1,0:T(8,128)(2,1)} %get-tuple-element.11), channel_id=1, source_target_pairs={{0,4},{1,5},{2,6},{3,7},{4,8},{5,9},{6,10},{7,11},{8,12},{9,13},{1... | collective-permute-start | bytes 294920 | tf_op jit(solution)/shard_map/ppermute | solution.py:307
  19.4 8.7 %collective-permute-start.2 = (bf16[48,1024]{1,0:T(8,128)(2,1)}, bf16[48,1024]{1,0:T(8,128)(2,1)S(1)}, u32[]{:S(2)}, u32[]{:S(2)}) collective-permute-start(bf16[48,1024]{1,0:T(8,128)(2,1)} %get-tuple-element.11), channel_id=1, source_target_pairs={{0,8},{1,9},{2,10},{3,11},{4,12},{5,13},{6,14},{7,15},{8,0},{9,1},... | collective-permute-start | bytes 294920 | tf_op jit(solution)/shard_map/ppermute | solution.py:307
  22.0 7.6 %collective-permute-start.3 = (bf16[48,1024]{1,0:T(8,128)(2,1)}, bf16[48,1024]{1,0:T(8,128)(2,1)S(1)}, u32[]{:S(2)}, u32[]{:S(2)}) collective-permute-start(bf16[48,1024]{1,0:T(8,128)(2,1)} %get-tuple-element.11), channel_id=1, source_target_pairs={{0,12},{1,13},{2,14},{3,15},{4,0},{5,1},{6,2},{7,3},{8,4},{9,5},{1... | collective-permute-start | bytes 294920 | tf_op jit(solution)/shard_map/ppermute | solution.py:307
  23.3 6.9 %collective-permute-start.4 = (bf16[48,1024]{1,0:T(8,128)(2,1)}, bf16[48,1024]{1,0:T(8,128)(2,1)S(1)}, u32[]{:S(2)}, u32[]{:S(2)}) collective-permute-start(bf16[48,1024]{1,0:T(8,128)(2,1)} %get-tuple-element.11), channel_id=1, source_target_pairs={{0,2},{1,3},{2,0},{3,1},{4,6},{5,7},{6,4},{7,5},{8,10},{9,11},{10,... | collective-permute-start | bytes 294920 | tf_op jit(solution)/shard_map/ppermute | solution.py:308
  25.7 4.9 %collective-permute-start.5 = (bf16[48,1024]{1,0:T(8,128)(2,1)S(1)}, bf16[48,1024]{1,0:T(8,128)(2,1)S(1)}, u32[]{:S(2)}, u32[]{:S(2)}) collective-permute-start(bf16[48,1024]{1,0:T(8,128)(2,1)S(1)} %collective-permute-done.1), channel_id=1, source_target_pairs={{0,2},{1,3},{2,0},{3,1},{4,6},{5,7},{6,4},{7,5},{8,10},{9,11},{10,... | collective-permute-start | bytes 294920 | tf_op jit(solution)/shard_map/ppermute | solution.py:308
  28.1 5.6 %collective-permute-start.6 = (bf16[48,1024]{1,0:T(8,128)(2,1)S(1)}, bf16[48,1024]{1,0:T(8,128)(2,1)S(1)}, u32[]{:S(2)}, u32[]{:S(2)}) collective-permute-start(bf16[48,1024]{1,0:T(8,128)(2,1)S(1)} %collective-permute-done.2), channel_id=1, source_target_pairs={{0,2},{1,3},{2,0},{3,1},{4,6},{5,7},{6,4},{7,5},{8,10},{9,11},{10,... | collective-permute-start | bytes 294920 | tf_op jit(solution)/shard_map/ppermute | solution.py:308
  29.6 5.1 %collective-permute-start.7 = (bf16[48,1024]{1,0:T(8,128)(2,1)S(1)}, bf16[48,1024]{1,0:T(8,128)(2,1)S(1)}, u32[]{:S(2)}, u32[]{:S(2)}) collective-permute-start(bf16[48,1024]{1,0:T(8,128)(2,1)S(1)} %collective-permute-done.3), channel_id=1, source_target_pairs={{0,2},{1,3},{2,0},{3,1},{4,6},{5,7},{6,4},{7,5},{8,10},{9,11},{10,... | collective-permute-start | bytes 294920 | tf_op jit(solution)/shard_map/ppermute | solution.py:308
  34.7 2.4 %collective-permute-start.8 = (bf16[384,1024]{1,0:T(8,128)(2,1)S(1)}, bf16[384,1024]{1,0:T(8,128)(2,1)S(1)}, u32[]{:S(2)}, u32[]{:S(2)}) collective-permute-start(bf16[384,1024]{1,0:T(8,128)(2,1)S(1)} %constant_dynamic-update-slice_fusion), channel_id=1, source_target_pairs={{0,1},{1,0},{2,3},{3,2},{4,5},{5,4},{6,7},{7,6},{8,9},{9,8},{10,11... | collective-permute-start | bytes 2359304 | tf_op jit(solution)/shard_map/ppermute | solution.py:310

commit v3 on v2

--- a/solution.py
+++ b/solution.py
@@ -123,8 +123,9 @@
     return jnp.broadcast_to(value[row : row + 1, :], (SUB, LANES))
 
 
-def lane_spread(value, lane):
-    return jnp.broadcast_to(value[:, lane : lane + 1], (SUB, LANES))
+def lane_spread(value, index, lane):
+    kept = jnp.where(lane == index, value, 0.0)
+    return jnp.broadcast_to(jnp.sum(kept, axis=1, keepdims=True), (SUB, LANES))
 
 
 def tree_sum(terms):
@@ -138,14 +139,24 @@
 
 
 def invert_rows(real_cols, imag_cols, rows, turned, sub):
-    scale = None
+    recip = 1.0 / spread(real_cols[0], 0)
+    scale = recip
     for j in range(SUB):
-        recip = 1.0 / spread(real_cols[j], j)
         own = sub == j
-        scale = recip if scale is None else jnp.where(own, recip, scale)
-        sr = jnp.where(own, 0.0, real_cols[j] * recip)
-        si = jnp.where(own, 0.0, imag_cols[j] * recip)
-        for l in range(j + 1, SUB):
+        if j:
+            scale = jnp.where(own, recip, scale)
+        cr = jnp.where(own, 0.0, real_cols[j])
+        ci = jnp.where(own, 0.0, imag_cols[j])
+        following = None
+        if j + 1 < SUB:
+            ur = spread(real_cols[j + 1], j)
+            ui = spread(imag_cols[j + 1], j)
+            real_cols[j + 1] = real_cols[j + 1] - (cr * ur - ci * ui) * recip
+            imag_cols[j + 1] = imag_cols[j + 1] - (cr * ui + ci * ur) * recip
+            following = 1.0 / spread(real_cols[j + 1], j + 1)
+        sr = cr * recip
+        si = ci * recip
+        for l in range(j + 2, SUB):
             ur = spread(real_cols[l], j)
             ui = spread(imag_cols[l], j)
             real_cols[l] = real_cols[l] - (sr * ur - si * ui)
@@ -154,18 +165,21 @@
         two = spread(turned, j)
         rows = rows - (sr * one + si * two)
         turned = turned - (sr * two - si * one)
+        recip = following
     return rows * scale, turned * scale
 
 
-def invert_block(tiles, lane, sub, sign):
+def invert_block(tiles, lane, sub, sign, hook):
     count = len(tiles)
     for t in range(count):
         k = SUB * t
         in_re = (lane >= k) & (lane < k + SUB)
         in_im = (lane >= HALF + k) & (lane < HALF + k + SUB)
         inside = in_re | in_im
-        real_cols = [lane_spread(tiles[t], k + l) for l in range(SUB)]
-        imag_cols = [lane_spread(tiles[t], HALF + k + l) for l in range(SUB)]
+        real_cols, imag_cols = [], []
+        for l in range(SUB):
+            real_cols.append(lane_spread(tiles[t], k + l, lane))
+            imag_cols.append(lane_spread(tiles[t], HALF + k + l, lane))
         unit = jnp.where(in_re & (lane - k == sub), 1.0, 0.0)
         rows = jnp.where(inside, unit, tiles[t])
         turned = pltpu.roll(rows, HALF, 1) * sign
@@ -177,11 +191,12 @@
         for i in list(range(t + 1, count)) + list(range(t)):
             terms = []
             for l in range(SUB):
-                cr = lane_spread(tiles[i], k + l)
-                ci = lane_spread(tiles[i], HALF + k + l)
+                cr = lane_spread(tiles[i], k + l, lane)
+                ci = lane_spread(tiles[i], HALF + k + l, lane)
                 terms.append(cr * ones[l] + ci * twos[l])
             fresh[i] = jnp.where(inside, 0.0, tiles[i]) - tree_sum(terms)
         tiles = fresh
+        hook(t)
     return tiles
 
 
@@ -198,8 +213,16 @@
     return jnp.dot(a, b, precision=HIGH, preferred_element_type=jnp.float32)
 
 
-def solve_kernel(train_count, beams, gram_ref, steer_ref, spec_ref, out_ref, mat, xs):
-    blocks = gram_ref.shape[0] // LANES
+def three(value):
+    high = value.astype(jnp.bfloat16)
+    rest = value - high.astype(jnp.float32)
+    mid = rest.astype(jnp.bfloat16)
+    return high, mid, (rest - mid.astype(jnp.float32)).astype(jnp.bfloat16)
+
+
+def solve_kernel(train_count, beams, steer_ref, spec_ref, *refs):
+    *side_refs, out_ref, mat, left6, right6, next6, under = refs
+    blocks = mat.shape[0] // HALF
     lane = lax.broadcasted_iota(jnp.int32, (SUB, LANES), 1)
     sub = lax.broadcasted_iota(jnp.int32, (SUB, LANES), 0)
     sign = jnp.where(lane < HALF, -1.0, 1.0)
@@ -209,11 +232,17 @@
     inv = 1.0 / train_count
     diag = blane == brow
     trace = jnp.zeros((HALF, LANES), jnp.float32)
+    contract = (((0,), (0,)), ((), ()))
     for i in range(blocks):
+        gram = None
+        for side in side_refs:
+            term = lax.dot_general(
+                side[:, i * LANES : (i + 1) * LANES], side[...], contract, preferred_element_type=jnp.float32
+            )
+            gram = term if gram is None else gram + term
         for j in range(blocks):
-            top = gram_ref[i * LANES : i * LANES + HALF, j * LANES : (j + 1) * LANES]
-            low = gram_ref[i * LANES + HALF : (i + 1) * LANES, j * LANES : (j + 1) * LANES]
-            value = (pltpu.roll(low, HALF, 1) - top * bsign) * inv
+            tile = gram[:, j * LANES : (j + 1) * LANES]
+            value = (pltpu.roll(tile[HALF:], HALF, 1) - tile[:HALF] * bsign) * inv
             mat[i * HALF : (i + 1) * HALF, j * LANES : (j + 1) * LANES] = value
             if i == j:
                 trace = trace + jnp.where(diag, value, 0.0)
@@ -223,40 +252,112 @@
         at = (slice(i * HALF, (i + 1) * HALF), slice(i * LANES, (i + 1) * LANES))
         mat[at] = mat[at] + jnp.where(diag, load, 0.0)
 
-    norm = jnp.zeros((HALF, LANES), jnp.float32)
+    norms = []
+    pivot = mat[0:HALF, 0:LANES]
+    ahead = {}
+    jobs = [lambda: prepare(0)]
+
+    def prepare(k):
+        start = (k + 1) * LANES
+        tile = mat[k * HALF : (k + 1) * HALF, start : start + LANES]
+        turned = turn(tile, bsign)
+        wide = jnp.concatenate(
+            [jnp.concatenate([tile, turned], 1), jnp.concatenate([turned, -tile], 1)], 0
+        )
+        high, mid, low = three(wide)
+        for place, part in enumerate((high, high, mid, mid, low, high)):
+            next6[place * LANES : (place + 1) * LANES, :] = part
+        if k + 1 < blocks:
+            high, mid, low = three(mat[(k + 1) * HALF : (k + 2) * HALF, k * LANES : start])
+            for place, part in enumerate((high, mid, high, low)):
+                under[:, place * LANES : (place + 1) * LANES] = part
+
+    def split_left(k, inverse):
+        whole = jnp.concatenate([inverse, turn(inverse, bsign)], 0)
+        scaled = exact_dot(mat[:, k * LANES : (k + 1) * LANES], whole)
+        pieces = [scaled[: k * HALF], inverse, scaled[(k + 1) * HALF :]]
+        scaled = jnp.concatenate(pieces if k else pieces[1:], 0)
+        high, mid, low = three(scaled)
+        for place, part in enumerate((high, mid, high, mid, high, low)):
+            left6[:, place * LANES : (place + 1) * LANES] = part
+
+    def split_right(k, tile):
+        at = slice(tile * LANES, (tile + 1) * LANES)
+        right = mat[k * HALF : (k + 1) * HALF, at]
+        high, mid, low = three(jnp.concatenate([right, turn(right, bsign)], 0))
+        for place, part in enumerate((high, high, mid, mid, low, high)):
+            right6[place * LANES : (place + 1) * LANES, at] = part
+
+    def update(k, tile, count):
+        own = slice(k * HALF, (k + 1) * HALF)
+        at = slice(tile * LANES, (tile + count) * LANES)
+        change = jnp.dot(left6[...], right6[:, at], preferred_element_type=jnp.float32)
+        if tile + count > blocks:
+            norms.append(mat[own, blocks * LANES :] * change[own, -LANES:])
+        if k:
+            mat[: k * HALF, at] = mat[: k * HALF, at] - change[: k * HALF]
+        mat[own, at] = change[own]
+        below = slice((k + 1) * HALF, None)
+        mat[below, at] = mat[below, at] - change[below]
+
+    def packed_dot(pairs):
+        out = None
+        for a, b in pairs:
+            term = jnp.dot(a, b, preferred_element_type=jnp.float32)
+            out = term if out is None else out + term
+        return out
+
     for k in range(blocks):
-        rows = slice(k * HALF, (k + 1) * HALF)
-        tiles = [
-            mat[k * HALF + SUB * t : k * HALF + SUB * (t + 1), k * LANES : (k + 1) * LANES]
-            for t in range(HALF // SUB)
-        ]
-        inverse = jnp.concatenate(invert_block(tiles, lane, sub, sign), 0)
-        right = mat[rows, (k + 1) * LANES :]
-        upper = exact_dot(inverse, jnp.concatenate([right, turn(right, bsign)], 0))
-        norm = norm + right[:, -LANES:] * upper[:, -LANES:]
-        mat[rows, (k + 1) * LANES :] = upper
+        tiles = [pivot[SUB * t : SUB * (t + 1)] for t in range(HALF // SUB)]
+        panels = HALF // SUB
+
+        def hook(t, jobs=jobs):
+            for job in jobs[t * len(jobs) // panels : (t + 1) * len(jobs) // panels]:
+                job()
+
+        inverse = jnp.concatenate(invert_block(tiles, lane, sub, sign, hook), 0)
+        start = (k + 1) * LANES
+        high, mid, low = three(inverse)
+        upper = jnp.concatenate([high, mid], 1)
+        lower = jnp.concatenate([high, low], 1)
+        first = packed_dot(
+            [
+                (upper, next6[0 : 2 * LANES, :]),
+                (upper, next6[2 * LANES : 4 * LANES, :]),
+                (lower, next6[4 * LANES :, :]),
+            ]
+        )
         if k + 1 < blocks:
-            below = slice((k + 1) * HALF, blocks * HALF)
-            both = jnp.concatenate([upper, turn(upper, bsign)], 0)
-            mat[below, (k + 1) * LANES :] = mat[below, (k + 1) * LANES :] - exact_dot(
-                mat[below, k * LANES : (k + 1) * LANES], both
+            high, mid, low = three(jnp.concatenate([first[:, :LANES], first[:, LANES:]], 0))
+            wide = jnp.concatenate([high, mid], 1)
+            change = jnp.dot(
+                under[:, : 2 * LANES], jnp.concatenate([wide, wide], 0), preferred_element_type=jnp.float32
             )
+            change = change[:, :LANES] + change[:, LANES:]
+            change = change + jnp.dot(
+                under[:, 2 * LANES :], jnp.concatenate([low, high], 0), preferred_element_type=jnp.float32
+            )
+            pivot = mat[(k + 1) * HALF : (k + 2) * HALF, start : start + LANES] - change
+            jobs = [lambda k=k, inverse=inverse: split_left(k, inverse)]
+            for j in range(k + 1, blocks + 1, 2):
+                count = min(2, blocks + 1 - j)
+                for c in range(count):
+                    jobs.append(lambda k=k, j=j, c=c: split_right(k, j + c))
+                jobs.append(lambda k=k, j=j, count=count: update(k, j, count))
+            jobs.append(lambda k=k: prepare(k + 1))
+        else:
+            own = slice(k * HALF, (k + 1) * HALF)
+            norms.append(mat[own, start:] * first[:, :LANES])
+            mat[own, start:] = first[:, :LANES]
+            both = jnp.concatenate([first[:, :LANES], first[:, LANES:]], 0)
+            above = slice(0, k * HALF)
+            mat[above, start:] = mat[above, start:] - exact_dot(mat[above, k * LANES : start], both)
+    norm = tree_sum(norms)
     total = jnp.sum(norm, axis=0, keepdims=True)
     total = total + pltpu.roll(jnp.broadcast_to(total, (SUB, LANES)), HALF, 1)[:1]
     low8 = (blane[:1] % HALF) < beams
     factor = jnp.where(low8, lax.rsqrt(jnp.where(low8, total, 1.0)), 0.0)
-    for k in reversed(range(blocks)):
-        rows = slice(k * HALF, (k + 1) * HALF)
-        value = mat[rows, blocks * LANES :]
-        if k + 1 < blocks:
-            value = value - exact_dot(
-                mat[rows, (k + 1) * LANES : blocks * LANES], xs[(k + 1) * LANES : blocks * LANES, :]
-            )
-        xs[k * LANES : k * LANES + HALF, :] = value
-        xs[k * LANES + HALF : (k + 1) * LANES, :] = turn(value, bsign)
-    weights = jnp.concatenate(
-        [(xs[k * LANES : k * LANES + HALF, :] * factor).astype(jnp.bfloat16) for k in range(blocks)], 0
-    )
+    weights = (mat[:, blocks * LANES :] * factor).astype(jnp.bfloat16)
     contract = (((0,), (1,)), ((), ()))
     real = lax.dot_general(weights, spec_ref[0], contract, preferred_element_type=jnp.float32)
     imag = lax.dot_general(weights, spec_ref[1], contract, preferred_element_type=jnp.float32)
@@ -264,18 +365,22 @@
     out_ref[1] = real[HALF : HALF + beams] - imag[:beams]
 
 
-def solve_and_filter(gram, steer, spectrum, train_count, beams):
-    channels = gram.shape[0] // 2
+def solve_and_filter(sides, steer, spectrum, train_count, beams):
+    channels = sides[0].shape[1] // 2
     gates = spectrum.shape[1]
+    width = 2 * channels + LANES
     return pl.pallas_call(
         lambda *refs: solve_kernel(train_count, beams, *refs),
         out_shape=jax.ShapeDtypeStruct((2, beams, gates), jnp.float32),
         scratch_shapes=[
-            pltpu.VMEM((channels, 2 * channels + LANES), jnp.float32),
-            pltpu.VMEM((2 * channels, LANES), jnp.float32),
+            pltpu.VMEM((channels, width), jnp.float32),
+            pltpu.VMEM((channels, 6 * LANES), jnp.bfloat16),
+            pltpu.VMEM((6 * LANES, width), jnp.bfloat16),
+            pltpu.VMEM((6 * LANES, 2 * LANES), jnp.bfloat16),
+            pltpu.VMEM((HALF, 4 * LANES), jnp.bfloat16),
         ],
         name="solve_and_filter",
-    )(gram, steer, spectrum)
+    )(steer, spectrum, *sides)
 
 
 def packed_steering(look_row, channels, angle_count):
@@ -324,14 +429,9 @@
         pairs = [(d, (d + hop) % dop) for d in range(dop)]
         mine.append(lax.ppermute(parts[hop], "dop", pairs))
     spectrum, packed = finish_spectra(train_gates, mine, 1.0 / math.sqrt(pulses))
-    gram = None
-    for side in gather_rows(packed, rng):
-        term = lax.dot_general(
-            side, side, (((0,), (0,)), ((), ())), preferred_element_type=jnp.float32
-        )
-        gram = term if gram is None else gram + term
+    sides = gather_rows(packed, rng)
     steer = packed_steering(look_angles[0], channels, NANG)
-    out = solve_and_filter(gram, steer, spectrum, train_gates.shape[1] * rng, beams)
+    out = solve_and_filter(sides, steer, spectrum, train_gates.shape[1] * rng, beams)
     return out[:, None]
 
 

time: 74.9 us -> 60.8 us (0.81)
  Pallas kernels: 40.4 us -> 30 us
  matrix products: 4.57 us -> 0 us
  local copies, waits for them, and re-layouts: 1.69 us -> 2.62 us
    pallas_call x1, Pallas kernels: 33.1 us -> 22.6 us  [solve_and_filter(): pl.pallas_call(lambda *refs: solve_kernel(train_count, beams, *refs), out...]
    dot_general x2 -> x0, matrix products: 4.57 us -> none  [on_device(): lax.dot_general(side, side, (((0,), (0,)), ((), ())), preferred_element_t...]
    unnamed x11 -> x15, local copies, waits for them, and re-layouts: 1.68 us -> 2.61 us
  transfers between devices with their start and end apart: 9 -> 9, of which waited for: 6 -> 6; matrix products, arithmetic and copies ran while one was open for 4% -> 5% of each run, Pallas kernels for 0% -> 0%
where the time goes in v3:
time: 60.8 us; the launch traced here: 60.6 us
  Pallas kernels  30 us (49%)
  starting transfers between devices  13.7 us (23%)
  waiting for transfers between devices  12.4 us (20%)
  local copies, waits for them, and re-layouts  2.62 us (4%)
  other arithmetic  1.79 us (3%)
    pallas_call x1, Pallas kernels, solve_and_filter(): pl.pallas_call(lambda *refs: solve_kernel(train_count, beams, *refs), out...  22.6 us
    ppermute x1, waiting for transfers between devices, on_device(): mine.append(lax.ppermute(parts[hop], 'dop', pairs))  6.51 us
    ppermute x3, starting transfers between devices, gather_rows(): pieces.append(lax.ppermute(rows, 'rng', shift_pairs(count, 4, outer, hop)))  5.74 us
    pallas_call x1, Pallas kernels, partial_spectra(): pl.pallas_call(lambda *refs: partial_kernel(classes, dop, table, *refs),...  5.5 us
    ppermute x4, starting transfers between devices, gather_rows(): lax.ppermute(piece, 'rng', shift_pairs(count, 2, 2, 1))  4.86 us
    ppermute x4, waiting for transfers between devices, gather_rows(): lax.ppermute(piece, 'rng', shift_pairs(count, 2, 2, 1))  4.45 us
    ppermute x1, starting transfers between devices, on_device(): mine.append(lax.ppermute(parts[hop], 'dop', pairs))  3 us
    unnamed x15, local copies, waits for them, and re-layouts  2.61 us
  transfers between devices with their start and end apart: 9, of which 6 were waited for; matrix products, arithmetic and copies ran while one was open for 5% of the time, Pallas kernels for 0%

profile of v3, /device:TPU:0, one launch (start us, length us, event | category | flops | bytes accessed | tf_op | source)
XLA Modules:
  0.0 60.6 jit_solution(12833294826175921071)
XLA Ops:
  0.0 0.0 copy-start.3
  0.0 5.5 %partial_spectra.1 = (f32[2,64,512]{2,1,0:T(8,128)}, f32[2,64,512]{2,1,0:T(8,128)}) custom-call(bf16[2,64,64,512]{3,2,1,0:T(8,128)(2,1)} %refs_0_.2), custom_call_target="tpu_custom_call" | custom-call | tf_op jit(solution)/shard_map/partial_spectra/pallas_call | solution.py:68
  5.5 3.0 %collective-permute-start = (f32[2,64,512]{2,1,0:T(8,128)}, f32[2,64,512]{2,1,0:T(8,128)S(1)}, u32[]{:S(2)}, u32[]{:S(2)}) collective-permute-start(f32[2,64,512]{2,1,0:T(8,128)} %get-tuple-element.10), channel_id=1, source_target_pairs={{0,16},{16,0},{1,17},{17,1},{2,18},{18,2},{3,19},{19,3},{4,20},{20... | collective-permute-start | bytes 786440 | tf_op jit(solution)/shard_map/ppermute | solution.py:430
  8.5 6.5 %collective-permute-done.refs_2_ = f32[2,64,512]{2,1,0:T(8,128)S(1)} collective-permute-done((f32[2,64,512]{2,1,0:T(8,128)}, f32[2,64,512]{2,1,0:T(8,128)S(1)}, u32[]{:S(2)}, u32[]{:S(2)}) %collective-permute-start) | collective-permute-done | bytes 262176 | tf_op jit(solution)/shard_map/ppermute | solution.py:430
  15.0 0.0 copy-start.2
  15.0 0.7 %copy-done.2 = f32[2,64,512]{2,1,0:T(8,128)} copy-done((f32[2,64,512]{2,1,0:T(8,128)}, f32[2,64,512]{2,1,0:T(8,128)S(1)}, u32[]{:S(2)}) %copy-start.2) | copy-done | bytes 262168
  15.7 1.9 %finish_spectra.1 = (bf16[2,64,512]{2,1,0:T(8,128)(2,1)}, bf16[48,1024]{1,0:T(8,128)(2,1)}) custom-call(s32[1,48]{1,0:T(1,128)} %refs_0_.3, f32[2,64,512]{2,1,0:T(8,128)} %get-tuple-element.9.refs_1_, f32[2,64,512]{2,1,0:T(8,128)} %copy-done.2), custom_call_target="tpu_custom_call" | custom-call | tf_op jit(solution)/shard_map/finish_spectra/pallas_call | solution.py:112
  17.6 1.8 %collective-permute-start.1 = (bf16[48,1024]{1,0:T(8,128)(2,1)}, bf16[48,1024]{1,0:T(8,128)(2,1)S(1)}, u32[]{:S(2)}, u32[]{:S(2)}) collective-permute-start(bf16[48,1024]{1,0:T(8,128)(2,1)} %get-tuple-element.12), channel_id=1, source_target_pairs={{0,4},{1,5},{2,6},{3,7},{4,8},{5,9},{6,10},{7,11},{8,12},{9,13},{1... | collective-permute-start | bytes 294920 | tf_op jit(solution)/shard_map/ppermute | solution.py:412
  19.4 2.6 %collective-permute-start.2 = (bf16[48,1024]{1,0:T(8,128)(2,1)}, bf16[48,1024]{1,0:T(8,128)(2,1)S(1)}, u32[]{:S(2)}, u32[]{:S(2)}) collective-permute-start(bf16[48,1024]{1,0:T(8,128)(2,1)} %get-tuple-element.12), channel_id=1, source_target_pairs={{0,8},{1,9},{2,10},{3,11},{4,12},{5,13},{6,14},{7,15},{8,0},{9,1},... | collective-permute-start | bytes 294920 | tf_op jit(solution)/shard_map/ppermute | solution.py:412
  22.0 1.3 %collective-permute-start.3 = (bf16[48,1024]{1,0:T(8,128)(2,1)}, bf16[48,1024]{1,0:T(8,128)(2,1)S(1)}, u32[]{:S(2)}, u32[]{:S(2)}) collective-permute-start(bf16[48,1024]{1,0:T(8,128)(2,1)} %get-tuple-element.12), channel_id=1, source_target_pairs={{0,12},{1,13},{2,14},{3,15},{4,0},{5,1},{6,2},{7,3},{8,4},{9,5},{1... | collective-permute-start | bytes 294920 | tf_op jit(solution)/shard_map/ppermute | solution.py:412
  23.3 1.5 %collective-permute-start.4 = (bf16[48,1024]{1,0:T(8,128)(2,1)}, bf16[48,1024]{1,0:T(8,128)(2,1)S(1)}, u32[]{:S(2)}, u32[]{:S(2)}) collective-permute-start(bf16[48,1024]{1,0:T(8,128)(2,1)} %get-tuple-element.12), channel_id=1, source_target_pairs={{0,2},{1,3},{2,0},{3,1},{4,6},{5,7},{6,4},{7,5},{8,10},{9,11},{10,... | collective-permute-start | bytes 294920 | tf_op jit(solution)/shard_map/ppermute | solution.py:413
  24.8 0.9 %constant_dynamic-update-slice_fusion.7 = bf16[384,1024]{1,0:T(8,128)(2,1)S(1)} fusion(bf16[48,1024]{1,0:T(8,128)(2,1)} %get-tuple-element.12), kind=kLoop, calls=%fused_computation.15 | loop fusion | bytes 196608
  25.7 0.0 collective-permute-done.1
  25.8 1.3 %collective-permute-start.5 = (bf16[48,1024]{1,0:T(8,128)(2,1)S(1)}, bf16[48,1024]{1,0:T(8,128)(2,1)S(1)}, u32[]{:S(2)}, u32[]{:S(2)}) collective-permute-start(bf16[48,1024]{1,0:T(8,128)(2,1)S(1)} %collective-permute-done.1), channel_id=1, source_target_pairs={{0,2},{1,3},{2,0},{3,1},{4,6},{5,7},{6,4},{7,5},{8,10},{9,11},{10,... | collective-permute-start | bytes 294920 | tf_op jit(solution)/shard_map/ppermute | solution.py:413
  27.0 1.0 %collective-permute-done.2 = bf16[48,1024]{1,0:T(8,128)(2,1)S(1)} collective-permute-done((bf16[48,1024]{1,0:T(8,128)(2,1)}, bf16[48,1024]{1,0:T(8,128)(2,1)S(1)}, u32[]{:S(2)}, u32[]{:S(2)}) %collective-permute-start.2) | collective-permute-done | bytes 98336 | tf_op jit(solution)/shard_map/ppermute | solution.py:412
  28.1 1.5 %collective-permute-start.6 = (bf16[48,1024]{1,0:T(8,128)(2,1)S(1)}, bf16[48,1024]{1,0:T(8,128)(2,1)S(1)}, u32[]{:S(2)}, u32[]{:S(2)}) collective-permute-start(bf16[48,1024]{1,0:T(8,128)(2,1)S(1)} %collective-permute-done.2), channel_id=1, source_target_pairs={{0,2},{1,3},{2,0},{3,1},{4,6},{5,7},{6,4},{7,5},{8,10},{9,11},{10,... | collective-permute-start | bytes 294920 | tf_op jit(solution)/shard_map/ppermute | solution.py:413
  29.6 0.0 collective-permute-done.3
  29.6 0.6 collective-permute-start.7
  30.2 0.0 collective-permute-done.4
  30.2 0.5 collective-permute-done.5
  30.7 2.9 %collective-permute-done.6 = bf16[48,1024]{1,0:T(8,128)(2,1)S(1)} collective-permute-done((bf16[48,1024]{1,0:T(8,128)(2,1)S(1)}, bf16[48,1024]{1,0:T(8,128)(2,1)S(1)}, u32[]{:S(2)}, u32[]{:S(2)}) %collective-permute-start.6) | collective-permute-done | bytes 98336 | tf_op jit(solution)/shard_map/ppermute | solution.py:413
  33.6 1.0 %collective-permute-done.7 = bf16[48,1024]{1,0:T(8,128)(2,1)S(1)} collective-permute-done((bf16[48,1024]{1,0:T(8,128)(2,1)S(1)}, bf16[48,1024]{1,0:T(8,128)(2,1)S(1)}, u32[]{:S(2)}, u32[]{:S(2)}) %collective-permute-start.7) | collective-permute-done | bytes 98336 | tf_op jit(solution)/shard_map/ppermute | solution.py:413
  34.7 0.0 copy-start
  34.7 0.1 collective-permute-start.8
  34.8 0.0 copy-done.3
  34.8 0.1 compare_select_fusion
  34.9 1.7 %fusion.4.refs_0_ = f32[512,128]{1,0:T(8,128)} fusion(s32[128]{0:T(128)S(1)} %get-tuple-element.13, s32[128]{0:T(128)S(1)} %get-tuple-element.14, pred[128]{0:T(512)(128)(4,1)S(1)} %fusion.5), kind=kLoop, calls=%fused_computation.7 | loop fusion | flops 1048576 | bytes 263296 | tf_op jit(solution)/shard_map/jit(_where)/select_n | solution.py:395
  36.6 0.4 collective-permute-done.8.refs_3_
  37.0 0.0 copy-start.1
  37.0 0.0 copy-done
  37.1 0.9 %copy-done.1 = bf16[384,1024]{1,0:T(8,128)(2,1)} copy-done((bf16[384,1024]{1,0:T(8,128)(2,1)}, bf16[384,1024]{1,0:T(8,128)(2,1)S(1)}, u32[]{:S(2)}) %copy-start.1) | copy-done | bytes 786456
  38.0 22.6 %solve_and_filter.1 = f32[2,8,64]{2,1,0:T(8,128)} custom-call(f32[512,128]{1,0:T(8,128)} %fusion.4.refs_0_, bf16[2,64,512]{2,1,0:T(8,128)(2,1)} %get-tuple-element.11.refs_1_, bf16[384,1024]{1,0:T(8,128)(2,1)} %copy-done, bf16[384,1024]{1,0:T(8,128)(2,1)} %copy-done.1), custom_call_target="tpu_custom_call" | custom-call | tf_op jit(solution)/shard_map/solve_and_filter/pallas_call | solution.py:372
  (10 shorter events, 0.1 us)
Async XLA Ops:
  0.0 34.8 %copy-start.3 = (s32[1,8]{1,0:T(1,128)S(1)}, s32[1,8]{1,0:T(1,128)}, u32[]{:S(2)}) copy-start(s32[1,8]{1,0:T(1,128)} %param.5) | copy-start | bytes 100
  5.5 9.5 %collective-permute-start = (f32[2,64,512]{2,1,0:T(8,128)}, f32[2,64,512]{2,1,0:T(8,128)S(1)}, u32[]{:S(2)}, u32[]{:S(2)}) collective-permute-start(f32[2,64,512]{2,1,0:T(8,128)} %get-tuple-element.10), channel_id=1, source_target_pairs={{0,16},{16,0},{1,17},{17,1},{2,18},{18,2},{3,19},{19,3},{4,20},{20... | collective-permute-start | bytes 786440 | tf_op jit(solution)/shard_map/ppermute | solution.py:430
  15.0 0.7 %copy-start.2 = (f32[2,64,512]{2,1,0:T(8,128)}, f32[2,64,512]{2,1,0:T(8,128)S(1)}, u32[]{:S(2)}) copy-start(f32[2,64,512]{2,1,0:T(8,128)S(1)} %collective-permute-done.refs_2_) | copy-start | bytes 786436
  17.6 8.2 %collective-permute-start.1 = (bf16[48,1024]{1,0:T(8,128)(2,1)}, bf16[48,1024]{1,0:T(8,128)(2,1)S(1)}, u32[]{:S(2)}, u32[]{:S(2)}) collective-permute-start(bf16[48,1024]{1,0:T(8,128)(2,1)} %get-tuple-element.12), channel_id=1, source_target_pairs={{0,4},{1,5},{2,6},{3,7},{4,8},{5,9},{6,10},{7,11},{8,12},{9,13},{1... | collective-permute-start | bytes 294920 | tf_op jit(solution)/shard_map/ppermute | solution.py:412
  19.4 8.7 %collective-permute-start.2 = (bf16[48,1024]{1,0:T(8,128)(2,1)}, bf16[48,1024]{1,0:T(8,128)(2,1)S(1)}, u32[]{:S(2)}, u32[]{:S(2)}) collective-permute-start(bf16[48,1024]{1,0:T(8,128)(2,1)} %get-tuple-element.12), channel_id=1, source_target_pairs={{0,8},{1,9},{2,10},{3,11},{4,12},{5,13},{6,14},{7,15},{8,0},{9,1},... | collective-permute-start | bytes 294920 | tf_op jit(solution)/shard_map/ppermute | solution.py:412
  22.0 7.6 %collective-permute-start.3 = (bf16[48,1024]{1,0:T(8,128)(2,1)}, bf16[48,1024]{1,0:T(8,128)(2,1)S(1)}, u32[]{:S(2)}, u32[]{:S(2)}) collective-permute-start(bf16[48,1024]{1,0:T(8,128)(2,1)} %get-tuple-element.12), channel_id=1, source_target_pairs={{0,12},{1,13},{2,14},{3,15},{4,0},{5,1},{6,2},{7,3},{8,4},{9,5},{1... | collective-permute-start | bytes 294920 | tf_op jit(solution)/shard_map/ppermute | solution.py:412
  23.3 6.9 %collective-permute-start.4 = (bf16[48,1024]{1,0:T(8,128)(2,1)}, bf16[48,1024]{1,0:T(8,128)(2,1)S(1)}, u32[]{:S(2)}, u32[]{:S(2)}) collective-permute-start(bf16[48,1024]{1,0:T(8,128)(2,1)} %get-tuple-element.12), channel_id=1, source_target_pairs={{0,2},{1,3},{2,0},{3,1},{4,6},{5,7},{6,4},{7,5},{8,10},{9,11},{10,... | collective-permute-start | bytes 294920 | tf_op jit(solution)/shard_map/ppermute | solution.py:413
  25.8 4.9 %collective-permute-start.5 = (bf16[48,1024]{1,0:T(8,128)(2,1)S(1)}, bf16[48,1024]{1,0:T(8,128)(2,1)S(1)}, u32[]{:S(2)}, u32[]{:S(2)}) collective-permute-start(bf16[48,1024]{1,0:T(8,128)(2,1)S(1)} %collective-permute-done.1), channel_id=1, source_target_pairs={{0,2},{1,3},{2,0},{3,1},{4,6},{5,7},{6,4},{7,5},{8,10},{9,11},{10,... | collective-permute-start | bytes 294920 | tf_op jit(solution)/shard_map/ppermute | solution.py:413
  28.1 5.6 %collective-permute-start.6 = (bf16[48,1024]{1,0:T(8,128)(2,1)S(1)}, bf16[48,1024]{1,0:T(8,128)(2,1)S(1)}, u32[]{:S(2)}, u32[]{:S(2)}) collective-permute-start(bf16[48,1024]{1,0:T(8,128)(2,1)S(1)} %collective-permute-done.2), channel_id=1, source_target_pairs={{0,2},{1,3},{2,0},{3,1},{4,6},{5,7},{6,4},{7,5},{8,10},{9,11},{10,... | collective-permute-start | bytes 294920 | tf_op jit(solution)/shard_map/ppermute | solution.py:413
  29.6 5.1 %collective-permute-start.7 = (bf16[48,1024]{1,0:T(8,128)(2,1)S(1)}, bf16[48,1024]{1,0:T(8,128)(2,1)S(1)}, u32[]{:S(2)}, u32[]{:S(2)}) collective-permute-start(bf16[48,1024]{1,0:T(8,128)(2,1)S(1)} %collective-permute-done.3), channel_id=1, source_target_pairs={{0,2},{1,3},{2,0},{3,1},{4,6},{5,7},{6,4},{7,5},{8,10},{9,11},{10,... | collective-permute-start | bytes 294920 | tf_op jit(solution)/shard_map/ppermute | solution.py:413
  34.7 2.4 %copy-start = (bf16[384,1024]{1,0:T(8,128)(2,1)}, bf16[384,1024]{1,0:T(8,128)(2,1)S(1)}, u32[]{:S(2)}) copy-start(bf16[384,1024]{1,0:T(8,128)(2,1)S(1)} %constant_dynamic-update-slice_fusion.refs_2_) | copy-start | bytes 2359300
  34.7 2.4 %collective-permute-start.8 = (bf16[384,1024]{1,0:T(8,128)(2,1)S(1)}, bf16[384,1024]{1,0:T(8,128)(2,1)S(1)}, u32[]{:S(2)}, u32[]{:S(2)}) collective-permute-start(bf16[384,1024]{1,0:T(8,128)(2,1)S(1)} %constant_dynamic-update-slice_fusion.refs_2_), channel_id=1, source_target_pairs={{0,1},{1,0},{2,3},{3,2},{4,5},{5,4},{6,7},{7,6},{8,9},{9,8},{10,11... | collective-permute-start | bytes 2359304 | tf_op jit(solution)/shard_map/ppermute | solution.py:415
  37.0 0.9 %copy-start.1 = (bf16[384,1024]{1,0:T(8,128)(2,1)}, bf16[384,1024]{1,0:T(8,128)(2,1)S(1)}, u32[]{:S(2)}) copy-start(bf16[384,1024]{1,0:T(8,128)(2,1)S(1)} %collective-permute-done.8.refs_3_) | copy-start | bytes 2359300

commit v4 on v3

--- a/solution.py
+++ b/solution.py
@@ -37,40 +37,59 @@
 
 
 def partial_kernel(classes, dop, table, *refs):
-    cube_ref, *out_refs = refs
+    cube_ref, *out_refs, buf, sems = refs
     me = lax.axis_index("dop")
-    local, _, width = cube_ref.shape[1:]
-    for base in range(0, width, LANES):
-        cols = slice(base, base + LANES)
-        folded = []
-        for part in range(2):
-            for cls in range(classes):
-                total = cube_ref[part, cls, :, cols].astype(jnp.float32)
-                for pulse in range(cls + classes, local, classes):
-                    total = total + cube_ref[part, pulse, :, cols].astype(jnp.float32)
-                folded.append(total)
-        for slot, out_ref in enumerate(out_refs):
-            for row in range(2):
-                acc = None
-                for part in range(2):
-                    for cls in range(classes):
-                        options = [
-                            table[row, (d + slot) % dop, part, d * local + cls] for d in range(dop)
-                        ]
-                        term = folded[part * classes + cls] * pick(options, me)
-                        acc = term if acc is None else acc + term
-                out_ref[row, :, cols] = acc
+    steps, _, local, step, width = buf.shape
+
+    def copy(n):
+        rows = pl.ds(pl.multiple_of(n * step, step), step)
+        return pltpu.make_async_copy(cube_ref.at[:, :, rows, :], buf.at[n], sems.at[n])
+
+    for n in range(steps):
+        copy(n).start()
+
+    def body(n, carry):
+        copy(n).wait()
+        rows = pl.ds(pl.multiple_of(n * step, step), step)
+        for base in range(0, width, LANES):
+            cols = slice(base, base + LANES)
+            folded = []
+            for part in range(2):
+                for cls in range(classes):
+                    total = buf[n, part, cls, :, cols].astype(jnp.float32)
+                    for pulse in range(cls + classes, local, classes):
+                        total = total + buf[n, part, pulse, :, cols].astype(jnp.float32)
+                    folded.append(total)
+            for slot, out_ref in enumerate(out_refs):
+                for row in range(2):
+                    acc = None
+                    for part in range(2):
+                        for cls in range(classes):
+                            options = [
+                                table[row, (d + slot) % dop, part, d * local + cls] for d in range(dop)
+                            ]
+                            term = folded[part * classes + cls] * pick(options, me)
+                            acc = term if acc is None else acc + term
+                    out_ref[row, rows, cols] = acc.astype(out_ref.dtype)
+        return carry
+
+    lax.fori_loop(0, steps, body, 0)
 
 
 def partial_spectra(cube, table, classes, dop):
     _, local, gates, channels = cube.shape
     step = 16
+    steps = gates // step
     return pl.pallas_call(
         lambda *refs: partial_kernel(classes, dop, table, *refs),
-        grid=(gates // step,),
-        in_specs=[pl.BlockSpec((2, local, step, channels), lambda i: (0, 0, i, 0))],
-        out_specs=[pl.BlockSpec((2, step, channels), lambda i: (0, i, 0))] * dop,
+        in_specs=[pl.BlockSpec(memory_space=pltpu.HBM)],
+        out_specs=[pl.BlockSpec(memory_space=pltpu.VMEM)] * dop,
         out_shape=[jax.ShapeDtypeStruct((2, gates, channels), jnp.float32)] * dop,
+        scratch_shapes=[
+            pltpu.VMEM((steps, 2, local, step, channels), cube.dtype),
+            pltpu.SemaphoreType.DMA((steps,)),
+        ],
+        compiler_params=pltpu.CompilerParams(vmem_limit_bytes=52 << 20),
         name="partial_spectra",
     )(cube)
 
@@ -115,6 +134,9 @@
             jax.ShapeDtypeStruct((2, gates, channels), jnp.bfloat16),
             jax.ShapeDtypeStruct((train, 2 * channels), jnp.bfloat16),
         ),
+        in_specs=[pl.BlockSpec(memory_space=pltpu.VMEM)] * (1 + len(parts)),
+        out_specs=[pl.BlockSpec(memory_space=pltpu.VMEM)] * 2,
+        compiler_params=pltpu.CompilerParams(vmem_limit_bytes=8 << 20),
         name="finish_spectra",
     )(gate_row, *parts)
 
@@ -372,6 +394,8 @@
     return pl.pallas_call(
         lambda *refs: solve_kernel(train_count, beams, *refs),
         out_shape=jax.ShapeDtypeStruct((2, beams, gates), jnp.float32),
+        in_specs=[pl.BlockSpec(memory_space=pltpu.VMEM)] * (2 + len(sides)),
+        out_specs=pl.BlockSpec(memory_space=pltpu.VMEM),
         scratch_shapes=[
             pltpu.VMEM((channels, width), jnp.float32),
             pltpu.VMEM((channels, 6 * LANES), jnp.bfloat16),
@@ -379,6 +403,7 @@
             pltpu.VMEM((6 * LANES, 2 * LANES), jnp.bfloat16),
             pltpu.VMEM((HALF, 4 * LANES), jnp.bfloat16),
         ],
+        compiler_params=pltpu.CompilerParams(vmem_limit_bytes=24 << 20),
         name="solve_and_filter",
     )(steer, spectrum, *sides)
 
@@ -407,12 +432,15 @@
     if count % 4:
         return (lax.all_gather(rows, "rng", axis=0, tiled=True),)
     outer = count // 4
+    swap = shift_pairs(count, 2, 2, 1)
+    pair = shift_pairs(count, 1, 2, 1)
+    across = [lax.ppermute(rows, "rng", swap)]
     pieces = [rows]
-    for hop in range(1, outer):
+    for hop in sorted(range(1, outer), key=lambda h: min(h, outer - h)):
         pieces.append(lax.ppermute(rows, "rng", shift_pairs(count, 4, outer, hop)))
-    across = [lax.ppermute(piece, "rng", shift_pairs(count, 2, 2, 1)) for piece in pieces]
+    across += [lax.ppermute(piece, "rng", swap) for piece in pieces[1:]]
     side = jnp.concatenate(pieces + across, 0)
-    return side, lax.ppermute(side, "rng", shift_pairs(count, 1, 2, 1))
+    return side, lax.ppermute(side, "rng", pair)
 
 
 def on_device(radar_cube, train_gates, look_angles):

time: 60.8 us -> 53.9 us (0.89)
  Pallas kernels: 30 us -> 25.3 us
  local copies, waits for them, and re-layouts: 2.62 us -> 0.07 us
  waiting for transfers between devices: 12.4 us -> 14.1 us
  other arithmetic: 1.79 us -> 1.07 us
    ppermute x3, waiting for transfers between devices: 1.03 us -> 3.63 us  [gather_rows(): pieces.append(lax.ppermute(rows, 'rng', shift_pairs(count, 4, outer, hop)))]
    unnamed x15 -> x11, local copies, waits for them, and re-layouts: 2.61 us -> 0.06 us
    pallas_call x1, Pallas kernels: 1.87 us -> 0.19 us  [finish_spectra(): pl.pallas_call(lambda *refs: finish_kernel(scale, *refs), out_shape=(jax....]
    pallas_call x1, Pallas kernels: 5.5 us -> 3.99 us  [partial_spectra(): pl.pallas_call(lambda *refs: partial_kernel(classes, dop, table, *refs),...]
    pallas_call x1, Pallas kernels: 22.6 us -> 21.1 us  [solve_and_filter(): pl.pallas_call(lambda *refs: solve_kernel(train_count, beams, *refs), out...]
    ppermute x3, starting transfers between devices: 5.74 us -> 4.89 us  [gather_rows(): pieces.append(lax.ppermute(rows, 'rng', shift_pairs(count, 4, outer, hop)))]
    ppermute x5, waiting for transfers between devices: 4.9 us -> 4.15 us  [the longest x3 2.99 us: gather_rows(): across += [lax.ppermute(piece, 'rng', swap) for piece in pieces[1:]]]
    select_n x1, other arithmetic: 1.7 us -> 0.99 us  [packed_steering(): return jnp.where((lane % HALF < beams)[None, :], value, 0.0)]
  transfers between devices with their start and end apart: 9 -> 9, of which waited for: 6 -> 6; matrix products, arithmetic and copies ran while one was open for 5% -> 2% of each run, Pallas kernels for 0% -> 0%
where the time goes in v4:
time: 53.9 us; the launch traced here: 53.8 us
  Pallas kernels  25.3 us (47%)
  waiting for transfers between devices  14.1 us (26%)
  starting transfers between devices  13.2 us (24%)
  other arithmetic  1.07 us (2%)
    pallas_call x1, Pallas kernels, solve_and_filter(): pl.pallas_call(lambda *refs: solve_kernel(train_count, beams, *refs), out...  21.1 us
    ppermute x1, waiting for transfers between devices, on_device(): mine.append(lax.ppermute(parts[hop], 'dop', pairs))  6.31 us
    ppermute x3, starting transfers between devices, gather_rows(): pieces.append(lax.ppermute(rows, 'rng', shift_pairs(count, 4, outer, hop)))  4.89 us
    pallas_call x1, Pallas kernels, partial_spectra(): pl.pallas_call(lambda *refs: partial_kernel(classes, dop, table, *refs),...  3.99 us
    ppermute x3, starting transfers between devices, gather_rows(): across += [lax.ppermute(piece, 'rng', swap) for piece in pieces[1:]]  3.65 us
    ppermute x3, waiting for transfers between devices, gather_rows(): pieces.append(lax.ppermute(rows, 'rng', shift_pairs(count, 4, outer, hop)))  3.63 us
    ppermute x1, starting transfers between devices, on_device(): mine.append(lax.ppermute(parts[hop], 'dop', pairs))  3.06 us
    ppermute x3, waiting for transfers between devices, gather_rows(): across += [lax.ppermute(piece, 'rng', swap) for piece in pieces[1:]]  2.99 us
  transfers between devices with their start and end apart: 9, of which 6 were waited for; matrix products, arithmetic and copies ran while one was open for 2% of the time, Pallas kernels for 0%

profile of v4, /device:TPU:0, one launch (start us, length us, event | category | flops | bytes accessed | tf_op | source)
XLA Modules:
  0.0 53.8 jit_solution(1035463557165194358)
XLA Ops:
  0.0 0.0 copy-start
  0.0 0.0 copy-start.1
  0.0 4.0 %partial_spectra.1 = (f32[2,64,512]{2,1,0:T(8,128)S(1)}, f32[2,64,512]{2,1,0:T(8,128)S(1)}) custom-call(bf16[2,64,64,512]{3,2,1,0:T(8,128)(2,1)} %refs_0_.2), custom_call_target="tpu_custom_call" | custom-call | tf_op jit(solution)/shard_map/partial_spectra/pallas_call | solution.py:83
  4.0 3.1 %collective-permute-start = (f32[2,64,512]{2,1,0:T(8,128)S(1)}, f32[2,64,512]{2,1,0:T(8,128)S(1)}, u32[]{:S(2)}, u32[]{:S(2)}) collective-permute-start(f32[2,64,512]{2,1,0:T(8,128)S(1)} %get-tuple-element.10), channel_id=1, source_target_pairs={{0,16},{16,0},{1,17},{17,1},{2,18},{18,2},{3,19},{19,3},{4,20},{20... | collective-permute-start | bytes 786440 | tf_op jit(solution)/shard_map/ppermute | solution.py:458
  7.1 6.3 %collective-permute-done.refs_2_ = f32[2,64,512]{2,1,0:T(8,128)S(1)} collective-permute-done((f32[2,64,512]{2,1,0:T(8,128)S(1)}, f32[2,64,512]{2,1,0:T(8,128)S(1)}, u32[]{:S(2)}, u32[]{:S(2)}) %collective-permute-start) | collective-permute-done | bytes 262176 | tf_op jit(solution)/shard_map/ppermute | solution.py:458
  13.4 0.0 copy-done
  13.4 0.2 finish_spectra.1
  13.6 1.8 %collective-permute-start.1 = (bf16[48,1024]{1,0:T(8,128)(2,1)S(1)}, bf16[48,1024]{1,0:T(8,128)(2,1)S(1)}, u32[]{:S(2)}, u32[]{:S(2)}) collective-permute-start(bf16[48,1024]{1,0:T(8,128)(2,1)S(1)} %get-tuple-element.12), channel_id=1, source_target_pairs={{0,4},{1,5},{2,6},{3,7},{4,8},{5,9},{6,10},{7,11},{8,12},{9,13},{1... | collective-permute-start | bytes 294920 | tf_op jit(solution)/shard_map/ppermute | solution.py:440
  15.4 2.1 %collective-permute-start.2 = (bf16[48,1024]{1,0:T(8,128)(2,1)S(1)}, bf16[48,1024]{1,0:T(8,128)(2,1)S(1)}, u32[]{:S(2)}, u32[]{:S(2)}) collective-permute-start(bf16[48,1024]{1,0:T(8,128)(2,1)S(1)} %get-tuple-element.12), channel_id=1, source_target_pairs={{0,12},{1,13},{2,14},{3,15},{4,0},{5,1},{6,2},{7,3},{8,4},{9,5},{1... | collective-permute-start | bytes 294920 | tf_op jit(solution)/shard_map/ppermute | solution.py:440
  17.5 0.9 %collective-permute-start.3 = (bf16[48,1024]{1,0:T(8,128)(2,1)S(1)}, bf16[48,1024]{1,0:T(8,128)(2,1)S(1)}, u32[]{:S(2)}, u32[]{:S(2)}) collective-permute-start(bf16[48,1024]{1,0:T(8,128)(2,1)S(1)} %get-tuple-element.12), channel_id=1, source_target_pairs={{0,8},{1,9},{2,10},{3,11},{4,12},{5,13},{6,14},{7,15},{8,0},{9,1},... | collective-permute-start | bytes 294920 | tf_op jit(solution)/shard_map/ppermute | solution.py:440
  18.5 1.5 %collective-permute-start.4 = (bf16[48,1024]{1,0:T(8,128)(2,1)S(1)}, bf16[48,1024]{1,0:T(8,128)(2,1)S(1)}, u32[]{:S(2)}, u32[]{:S(2)}) collective-permute-start(bf16[48,1024]{1,0:T(8,128)(2,1)S(1)} %get-tuple-element.12), channel_id=1, source_target_pairs={{0,2},{1,3},{2,0},{3,1},{4,6},{5,7},{6,4},{7,5},{8,10},{9,11},{10,... | collective-permute-start | bytes 294920 | tf_op jit(solution)/shard_map/ppermute | solution.py:437
  20.0 1.2 %collective-permute-done.1 = bf16[48,1024]{1,0:T(8,128)(2,1)S(1)} collective-permute-done((bf16[48,1024]{1,0:T(8,128)(2,1)S(1)}, bf16[48,1024]{1,0:T(8,128)(2,1)S(1)}, u32[]{:S(2)}, u32[]{:S(2)}) %collective-permute-start.1) | collective-permute-done | bytes 98336 | tf_op jit(solution)/shard_map/ppermute | solution.py:440
  21.2 1.7 %collective-permute-start.5 = (bf16[48,1024]{1,0:T(8,128)(2,1)S(1)}, bf16[48,1024]{1,0:T(8,128)(2,1)S(1)}, u32[]{:S(2)}, u32[]{:S(2)}) collective-permute-start(bf16[48,1024]{1,0:T(8,128)(2,1)S(1)} %collective-permute-done.1), channel_id=1, source_target_pairs={{0,2},{1,3},{2,0},{3,1},{4,6},{5,7},{6,4},{7,5},{8,10},{9,11},{10,... | collective-permute-start | bytes 294920 | tf_op jit(solution)/shard_map/ppermute | solution.py:441
  22.9 0.0 collective-permute-done.2
  22.9 0.4 collective-permute-start.6
  23.3 2.4 %collective-permute-done.3 = bf16[48,1024]{1,0:T(8,128)(2,1)S(1)} collective-permute-done((bf16[48,1024]{1,0:T(8,128)(2,1)S(1)}, bf16[48,1024]{1,0:T(8,128)(2,1)S(1)}, u32[]{:S(2)}, u32[]{:S(2)}) %collective-permute-start.3) | collective-permute-done | bytes 98336 | tf_op jit(solution)/shard_map/ppermute | solution.py:440
  25.7 1.6 %collective-permute-start.7 = (bf16[48,1024]{1,0:T(8,128)(2,1)S(1)}, bf16[48,1024]{1,0:T(8,128)(2,1)S(1)}, u32[]{:S(2)}, u32[]{:S(2)}) collective-permute-start(bf16[48,1024]{1,0:T(8,128)(2,1)S(1)} %collective-permute-done.3), channel_id=1, source_target_pairs={{0,2},{1,3},{2,0},{3,1},{4,6},{5,7},{6,4},{7,5},{8,10},{9,11},{10,... | collective-permute-start | bytes 294920 | tf_op jit(solution)/shard_map/ppermute | solution.py:441
  27.3 0.0 collective-permute-done.4
  27.3 0.0 collective-permute-done.5
  27.3 0.9 %collective-permute-done.6 = bf16[48,1024]{1,0:T(8,128)(2,1)S(1)} collective-permute-done((bf16[48,1024]{1,0:T(8,128)(2,1)S(1)}, bf16[48,1024]{1,0:T(8,128)(2,1)S(1)}, u32[]{:S(2)}, u32[]{:S(2)}) %collective-permute-start.6) | collective-permute-done | bytes 98336 | tf_op jit(solution)/shard_map/ppermute | solution.py:441
  28.3 2.1 %collective-permute-done.7 = bf16[48,1024]{1,0:T(8,128)(2,1)S(1)} collective-permute-done((bf16[48,1024]{1,0:T(8,128)(2,1)S(1)}, bf16[48,1024]{1,0:T(8,128)(2,1)S(1)}, u32[]{:S(2)}, u32[]{:S(2)}) %collective-permute-start.7) | collective-permute-done | bytes 98336 | tf_op jit(solution)/shard_map/ppermute | solution.py:441
  30.3 0.1 collective-permute-start.8
  30.4 0.0 copy-done.1
  30.5 0.1 compare_select_fusion
  30.5 1.0 %fusion.4.refs_0_ = f32[512,128]{1,0:T(8,128)S(1)} fusion(s32[128]{0:T(128)S(1)} %get-tuple-element.13, s32[128]{0:T(128)S(1)} %get-tuple-element.14, pred[128]{0:T(512)(128)(4,1)S(1)} %fusion.5), kind=kLoop, calls=%fused_computation.7 | loop fusion | flops 1048576 | bytes 263296 | tf_op jit(solution)/shard_map/jit(_where)/select_n | solution.py:420
  31.5 1.2 %collective-permute-done.8.refs_3_ = bf16[384,1024]{1,0:T(8,128)(2,1)S(1)} collective-permute-done((bf16[384,1024]{1,0:T(8,128)(2,1)S(1)}, bf16[384,1024]{1,0:T(8,128)(2,1)S(1)}, u32[]{:S(2)}, u32[]{:S(2)}) %collective-permute-start.8) | collective-permute-done | bytes 786464 | tf_op jit(solution)/shard_map/ppermute | solution.py:443
  32.7 21.1 %solve_and_filter.1 = f32[2,8,64]{2,1,0:T(8,128)} custom-call(f32[512,128]{1,0:T(8,128)S(1)} %fusion.4.refs_0_, bf16[2,64,512]{2,1,0:T(8,128)(2,1)S(1)} %get-tuple-element.11.refs_1_, bf16[384,1024]{1,0:T(8,128)(2,1)S(1)} %constant_dynamic-update-slice_fusion.refs_2_, bf16[384,1024]{1,0:T(8,128)(2,1)S(1)} %collective-permute-done.8.refs_3_), custom_call_target="tpu_custom_call" | custom-call | tf_op jit(solution)/shard_map/solve_and_filter/pallas_call | solution.py:394
  (11 shorter events, 0.1 us)
Async XLA Ops:
  0.0 13.4 %copy-start = (s32[1,48]{1,0:T(1,128)S(1)}, s32[1,48]{1,0:T(1,128)}, u32[]{:S(2)}) copy-start(s32[1,48]{1,0:T(1,128)} %refs_0_.3) | copy-start | bytes 580
  0.0 30.4 %copy-start.1 = (s32[1,8]{1,0:T(1,128)S(1)}, s32[1,8]{1,0:T(1,128)}, u32[]{:S(2)}) copy-start(s32[1,8]{1,0:T(1,128)} %param.5) | copy-start | bytes 100
  4.0 9.4 %collective-permute-start = (f32[2,64,512]{2,1,0:T(8,128)S(1)}, f32[2,64,512]{2,1,0:T(8,128)S(1)}, u32[]{:S(2)}, u32[]{:S(2)}) collective-permute-start(f32[2,64,512]{2,1,0:T(8,128)S(1)} %get-tuple-element.10), channel_id=1, source_target_pairs={{0,16},{16,0},{1,17},{17,1},{2,18},{18,2},{3,19},{19,3},{4,20},{20... | collective-permute-start | bytes 786440 | tf_op jit(solution)/shard_map/ppermute | solution.py:458
  13.6 7.6 %collective-permute-start.1 = (bf16[48,1024]{1,0:T(8,128)(2,1)S(1)}, bf16[48,1024]{1,0:T(8,128)(2,1)S(1)}, u32[]{:S(2)}, u32[]{:S(2)}) collective-permute-start(bf16[48,1024]{1,0:T(8,128)(2,1)S(1)} %get-tuple-element.12), channel_id=1, source_target_pairs={{0,4},{1,5},{2,6},{3,7},{4,8},{5,9},{6,10},{7,11},{8,12},{9,13},{1... | collective-permute-start | bytes 294920 | tf_op jit(solution)/shard_map/ppermute | solution.py:440
  15.4 7.5 %collective-permute-start.2 = (bf16[48,1024]{1,0:T(8,128)(2,1)S(1)}, bf16[48,1024]{1,0:T(8,128)(2,1)S(1)}, u32[]{:S(2)}, u32[]{:S(2)}) collective-permute-start(bf16[48,1024]{1,0:T(8,128)(2,1)S(1)} %get-tuple-element.12), channel_id=1, source_target_pairs={{0,12},{1,13},{2,14},{3,15},{4,0},{5,1},{6,2},{7,3},{8,4},{9,5},{1... | collective-permute-start | bytes 294920 | tf_op jit(solution)/shard_map/ppermute | solution.py:440
  17.5 8.2 %collective-permute-start.3 = (bf16[48,1024]{1,0:T(8,128)(2,1)S(1)}, bf16[48,1024]{1,0:T(8,128)(2,1)S(1)}, u32[]{:S(2)}, u32[]{:S(2)}) collective-permute-start(bf16[48,1024]{1,0:T(8,128)(2,1)S(1)} %get-tuple-element.12), channel_id=1, source_target_pairs={{0,8},{1,9},{2,10},{3,11},{4,12},{5,13},{6,14},{7,15},{8,0},{9,1},... | collective-permute-start | bytes 294920 | tf_op jit(solution)/shard_map/ppermute | solution.py:440
  18.5 8.8 %collective-permute-start.4 = (bf16[48,1024]{1,0:T(8,128)(2,1)S(1)}, bf16[48,1024]{1,0:T(8,128)(2,1)S(1)}, u32[]{:S(2)}, u32[]{:S(2)}) collective-permute-start(bf16[48,1024]{1,0:T(8,128)(2,1)S(1)} %get-tuple-element.12), channel_id=1, source_target_pairs={{0,2},{1,3},{2,0},{3,1},{4,6},{5,7},{6,4},{7,5},{8,10},{9,11},{10,... | collective-permute-start | bytes 294920 | tf_op jit(solution)/shard_map/ppermute | solution.py:437
  21.2 6.1 %collective-permute-start.5 = (bf16[48,1024]{1,0:T(8,128)(2,1)S(1)}, bf16[48,1024]{1,0:T(8,128)(2,1)S(1)}, u32[]{:S(2)}, u32[]{:S(2)}) collective-permute-start(bf16[48,1024]{1,0:T(8,128)(2,1)S(1)} %collective-permute-done.1), channel_id=1, source_target_pairs={{0,2},{1,3},{2,0},{3,1},{4,6},{5,7},{6,4},{7,5},{8,10},{9,11},{10,... | collective-permute-start | bytes 294920 | tf_op jit(solution)/shard_map/ppermute | solution.py:441
  22.9 5.3 %collective-permute-start.6 = (bf16[48,1024]{1,0:T(8,128)(2,1)S(1)}, bf16[48,1024]{1,0:T(8,128)(2,1)S(1)}, u32[]{:S(2)}, u32[]{:S(2)}) collective-permute-start(bf16[48,1024]{1,0:T(8,128)(2,1)S(1)} %collective-permute-done.2), channel_id=1, source_target_pairs={{0,2},{1,3},{2,0},{3,1},{4,6},{5,7},{6,4},{7,5},{8,10},{9,11},{10,... | collective-permute-start | bytes 294920 | tf_op jit(solution)/shard_map/ppermute | solution.py:441
  25.7 4.6 %collective-permute-start.7 = (bf16[48,1024]{1,0:T(8,128)(2,1)S(1)}, bf16[48,1024]{1,0:T(8,128)(2,1)S(1)}, u32[]{:S(2)}, u32[]{:S(2)}) collective-permute-start(bf16[48,1024]{1,0:T(8,128)(2,1)S(1)} %collective-permute-done.3), channel_id=1, source_target_pairs={{0,2},{1,3},{2,0},{3,1},{4,6},{5,7},{6,4},{7,5},{8,10},{9,11},{10,... | collective-permute-start | bytes 294920 | tf_op jit(solution)/shard_map/ppermute | solution.py:441
  30.3 2.4 %collective-permute-start.8 = (bf16[384,1024]{1,0:T(8,128)(2,1)S(1)}, bf16[384,1024]{1,0:T(8,128)(2,1)S(1)}, u32[]{:S(2)}, u32[]{:S(2)}) collective-permute-start(bf16[384,1024]{1,0:T(8,128)(2,1)S(1)} %constant_dynamic-update-slice_fusion.refs_2_), channel_id=1, source_target_pairs={{0,1},{1,0},{2,3},{3,2},{4,5},{5,4},{6,7},{7,6},{8,9},{9,8},{10,11... | collective-permute-start | bytes 2359304 | tf_op jit(solution)/shard_map/ppermute | solution.py:443

commit v5 on v4

--- a/solution.py
+++ b/solution.py
@@ -7,6 +7,7 @@
 from jax.experimental import pallas as pl
 from jax.experimental.pallas import tpu as pltpu
 from jax.sharding import PartitionSpec as P
+
 
 NANG = 256
 LOAD_EPS = 1e-05
@@ -84,7 +85,10 @@
         lambda *refs: partial_kernel(classes, dop, table, *refs),
         in_specs=[pl.BlockSpec(memory_space=pltpu.HBM)],
         out_specs=[pl.BlockSpec(memory_space=pltpu.VMEM)] * dop,
-        out_shape=[jax.ShapeDtypeStruct((2, gates, channels), jnp.float32)] * dop,
+        out_shape=[
+            jax.ShapeDtypeStruct((2, gates, channels), jnp.float32)
+            for _ in range(dop)
+        ],
         scratch_shapes=[
             pltpu.VMEM((steps, 2, local, step, channels), cube.dtype),
             pltpu.SemaphoreType.DMA((steps,)),
@@ -112,7 +116,7 @@
         for part in range(2):
             total = parts[0][part, :, cols]
             for other in parts[1:]:
-                total = total + other[part, :, cols]
+                total = total + other[part, :, cols].astype(jnp.float32)
             value = (total * scale).astype(jnp.bfloat16)
             spec_ref[part, :, cols] = value
             value = value.astype(jnp.float32)
@@ -243,7 +247,7 @@
 
 
 def solve_kernel(train_count, beams, steer_ref, spec_ref, *refs):
-    *side_refs, out_ref, mat, left6, right6, next6, under = refs
+    *side_refs, out_ref, mat, left6, right6, next6, under, flipped = refs
     blocks = mat.shape[0] // HALF
     lane = lax.broadcasted_iota(jnp.int32, (SUB, LANES), 1)
     sub = lax.broadcasted_iota(jnp.int32, (SUB, LANES), 0)
@@ -253,31 +257,51 @@
     bsign = jnp.where(blane < HALF, -1.0, 1.0)
     inv = 1.0 / train_count
     diag = blane == brow
-    trace = jnp.zeros((HALF, LANES), jnp.float32)
-    contract = (((0,), (0,)), ((), ()))
-    for i in range(blocks):
-        gram = None
-        for side in side_refs:
-            term = lax.dot_general(
-                side[:, i * LANES : (i + 1) * LANES], side[...], contract, preferred_element_type=jnp.float32
+    train = side_refs[0].shape[0]
+    squares = jnp.zeros((1, LANES), jnp.float32)
+    for side in side_refs:
+        value = side[...].astype(jnp.float32)
+        sums = jnp.sum(value * value, axis=0, keepdims=True)
+        squares = squares + tree_sum([sums[:, j * LANES : (j + 1) * LANES] for j in range(blocks)])
+    load = jnp.sum(squares, axis=1, keepdims=True) * (LOAD_EPS * inv / (blocks * HALF))
+
+    def flip(i):
+        for place, side in enumerate(side_refs):
+            flipped[i * LANES : (i + 1) * LANES, place * train : (place + 1) * train] = side[
+                :, i * LANES : (i + 1) * LANES
+            ].T
+
+    def gram(rows, cols):
+        terms = [
+            jnp.dot(
+                flipped[rows, place * train : (place + 1) * train],
+                side[:, cols],
+                preferred_element_type=jnp.float32,
             )
-            gram = term if gram is None else gram + term
-        for j in range(blocks):
-            tile = gram[:, j * LANES : (j + 1) * LANES]
-            value = (pltpu.roll(tile[HALF:], HALF, 1) - tile[:HALF] * bsign) * inv
-            mat[i * HALF : (i + 1) * HALF, j * LANES : (j + 1) * LANES] = value
-            if i == j:
-                trace = trace + jnp.where(diag, value, 0.0)
-        mat[i * HALF : (i + 1) * HALF, blocks * LANES :] = steer_ref[i * HALF : (i + 1) * HALF, :]
-    load = LOAD_EPS * jnp.sum(trace, keepdims=True) / (blocks * HALF)
-    for i in range(blocks):
-        at = (slice(i * HALF, (i + 1) * HALF), slice(i * LANES, (i + 1) * LANES))
-        mat[at] = mat[at] + jnp.where(diag, load, 0.0)
-
+            for place, side in enumerate(side_refs)
+        ]
+        return tree_sum(terms)
+
+    def covariance(tile, on_diagonal):
+        value = (pltpu.roll(tile[HALF:], HALF, 1) - tile[:HALF] * bsign) * inv
+        return value + jnp.where(diag, load, 0.0) if on_diagonal else value
+
+    def fill(j, count):
+        tall = gram(slice(None), slice(j * LANES, (j + count) * LANES))
+        for c in range(count):
+            for i in range(blocks):
+                tile = tall[i * LANES : (i + 1) * LANES, c * LANES : (c + 1) * LANES]
+                mat[i * HALF : (i + 1) * HALF, (j + c) * LANES : (j + c + 1) * LANES] = covariance(
+                    tile, i == j + c
+                )
+
+    mat[:, blocks * LANES :] = steer_ref[...]
+    flip(0)
     norms = []
-    pivot = mat[0:HALF, 0:LANES]
-    ahead = {}
-    jobs = [lambda: prepare(0)]
+    pivot = covariance(gram(slice(0, LANES), slice(0, LANES)), True)
+    jobs = [lambda i=i: flip(i) for i in range(1, blocks)]
+    jobs += [lambda j=j: fill(j, min(2, blocks - j)) for j in range(0, blocks, 2)]
+    jobs.append(lambda: prepare(0))
 
     def prepare(k):
         start = (k + 1) * LANES
@@ -402,6 +426,7 @@
             pltpu.VMEM((6 * LANES, width), jnp.bfloat16),
             pltpu.VMEM((6 * LANES, 2 * LANES), jnp.bfloat16),
             pltpu.VMEM((HALF, 4 * LANES), jnp.bfloat16),
+            pltpu.VMEM((2 * channels, sum(side.shape[0] for side in sides)), jnp.bfloat16),
         ],
         compiler_params=pltpu.CompilerParams(vmem_limit_bytes=24 << 20),
         name="solve_and_filter",

time: 53.9 us -> 52.4 us (0.972)
  Pallas kernels: 25.3 us -> 23.8 us
    pallas_call x1, Pallas kernels: 21.1 us -> 19.6 us  [solve_and_filter(): pl.pallas_call(lambda *refs: solve_kernel(train_count, beams, *refs), out...]
where the time goes in v5:
time: 52.4 us; the launch traced here: 52.3 us
  Pallas kernels  23.8 us (45%)
  waiting for transfers between devices  14.1 us (27%)
  starting transfers between devices  13.2 us (25%)
  other arithmetic  1.07 us (2%)
    pallas_call x1, Pallas kernels, solve_and_filter(): pl.pallas_call(lambda *refs: solve_kernel(train_count, beams, *refs), out...  19.6 us
    ppermute x1, waiting for transfers between devices, on_device(): mine.append(lax.ppermute(parts[hop], 'dop', pairs))  6.31 us
    ppermute x3, starting transfers between devices, gather_rows(): pieces.append(lax.ppermute(rows, 'rng', shift_pairs(count, 4, outer, hop)))  4.89 us
    pallas_call x1, Pallas kernels, partial_spectra(): pl.pallas_call(lambda *refs: partial_kernel(classes, dop, table, *refs),...  3.99 us
    ppermute x3, starting transfers between devices, gather_rows(): across += [lax.ppermute(piece, 'rng', swap) for piece in pieces[1:]]  3.65 us
    ppermute x3, waiting for transfers between devices, gather_rows(): pieces.append(lax.ppermute(rows, 'rng', shift_pairs(count, 4, outer, hop)))  3.63 us
    ppermute x1, starting transfers between devices, on_device(): mine.append(lax.ppermute(parts[hop], 'dop', pairs))  3.06 us
    ppermute x3, waiting for transfers between devices, gather_rows(): across += [lax.ppermute(piece, 'rng', swap) for piece in pieces[1:]]  2.99 us
  transfers between devices with their start and end apart: 9, of which 6 were waited for; matrix products, arithmetic and copies ran while one was open for 2% of the time, Pallas kernels for 0%

profile of v5, /device:TPU:0, one launch (start us, length us, event | category | flops | bytes accessed | tf_op | source)
XLA Modules:
  0.0 52.3 jit_solution(7640409555950203758)
XLA Ops:
  0.0 0.0 copy-start
  0.0 0.0 copy-start.1
  0.0 4.0 %partial_spectra.1 = (f32[2,64,512]{2,1,0:T(8,128)S(1)}, f32[2,64,512]{2,1,0:T(8,128)S(1)}) custom-call(bf16[2,64,64,512]{3,2,1,0:T(8,128)(2,1)} %refs_0_.2), custom_call_target="tpu_custom_call" | custom-call | tf_op jit(solution)/shard_map/partial_spectra/pallas_call | solution.py:84
  4.0 3.1 %collective-permute-start = (f32[2,64,512]{2,1,0:T(8,128)S(1)}, f32[2,64,512]{2,1,0:T(8,128)S(1)}, u32[]{:S(2)}, u32[]{:S(2)}) collective-permute-start(f32[2,64,512]{2,1,0:T(8,128)S(1)} %get-tuple-element.10), channel_id=1, source_target_pairs={{0,16},{16,0},{1,17},{17,1},{2,18},{18,2},{3,19},{19,3},{4,20},{20... | collective-permute-start | bytes 786440 | tf_op jit(solution)/shard_map/ppermute | solution.py:483
  7.1 6.3 %collective-permute-done.refs_2_ = f32[2,64,512]{2,1,0:T(8,128)S(1)} collective-permute-done((f32[2,64,512]{2,1,0:T(8,128)S(1)}, f32[2,64,512]{2,1,0:T(8,128)S(1)}, u32[]{:S(2)}, u32[]{:S(2)}) %collective-permute-start) | collective-permute-done | bytes 262176 | tf_op jit(solution)/shard_map/ppermute | solution.py:483
  13.4 0.0 copy-done
  13.4 0.2 finish_spectra.1
  13.6 1.8 %collective-permute-start.1 = (bf16[48,1024]{1,0:T(8,128)(2,1)S(1)}, bf16[48,1024]{1,0:T(8,128)(2,1)S(1)}, u32[]{:S(2)}, u32[]{:S(2)}) collective-permute-start(bf16[48,1024]{1,0:T(8,128)(2,1)S(1)} %get-tuple-element.12), channel_id=1, source_target_pairs={{0,4},{1,5},{2,6},{3,7},{4,8},{5,9},{6,10},{7,11},{8,12},{9,13},{1... | collective-permute-start | bytes 294920 | tf_op jit(solution)/shard_map/ppermute | solution.py:465
  15.4 2.1 %collective-permute-start.2 = (bf16[48,1024]{1,0:T(8,128)(2,1)S(1)}, bf16[48,1024]{1,0:T(8,128)(2,1)S(1)}, u32[]{:S(2)}, u32[]{:S(2)}) collective-permute-start(bf16[48,1024]{1,0:T(8,128)(2,1)S(1)} %get-tuple-element.12), channel_id=1, source_target_pairs={{0,12},{1,13},{2,14},{3,15},{4,0},{5,1},{6,2},{7,3},{8,4},{9,5},{1... | collective-permute-start | bytes 294920 | tf_op jit(solution)/shard_map/ppermute | solution.py:465
  17.5 0.9 %collective-permute-start.3 = (bf16[48,1024]{1,0:T(8,128)(2,1)S(1)}, bf16[48,1024]{1,0:T(8,128)(2,1)S(1)}, u32[]{:S(2)}, u32[]{:S(2)}) collective-permute-start(bf16[48,1024]{1,0:T(8,128)(2,1)S(1)} %get-tuple-element.12), channel_id=1, source_target_pairs={{0,8},{1,9},{2,10},{3,11},{4,12},{5,13},{6,14},{7,15},{8,0},{9,1},... | collective-permute-start | bytes 294920 | tf_op jit(solution)/shard_map/ppermute | solution.py:465
  18.5 1.5 %collective-permute-start.4 = (bf16[48,1024]{1,0:T(8,128)(2,1)S(1)}, bf16[48,1024]{1,0:T(8,128)(2,1)S(1)}, u32[]{:S(2)}, u32[]{:S(2)}) collective-permute-start(bf16[48,1024]{1,0:T(8,128)(2,1)S(1)} %get-tuple-element.12), channel_id=1, source_target_pairs={{0,2},{1,3},{2,0},{3,1},{4,6},{5,7},{6,4},{7,5},{8,10},{9,11},{10,... | collective-permute-start | bytes 294920 | tf_op jit(solution)/shard_map/ppermute | solution.py:462
  20.0 1.2 %collective-permute-done.1 = bf16[48,1024]{1,0:T(8,128)(2,1)S(1)} collective-permute-done((bf16[48,1024]{1,0:T(8,128)(2,1)S(1)}, bf16[48,1024]{1,0:T(8,128)(2,1)S(1)}, u32[]{:S(2)}, u32[]{:S(2)}) %collective-permute-start.1) | collective-permute-done | bytes 98336 | tf_op jit(solution)/shard_map/ppermute | solution.py:465
  21.2 1.7 %collective-permute-start.5 = (bf16[48,1024]{1,0:T(8,128)(2,1)S(1)}, bf16[48,1024]{1,0:T(8,128)(2,1)S(1)}, u32[]{:S(2)}, u32[]{:S(2)}) collective-permute-start(bf16[48,1024]{1,0:T(8,128)(2,1)S(1)} %collective-permute-done.1), channel_id=1, source_target_pairs={{0,2},{1,3},{2,0},{3,1},{4,6},{5,7},{6,4},{7,5},{8,10},{9,11},{10,... | collective-permute-start | bytes 294920 | tf_op jit(solution)/shard_map/ppermute | solution.py:466
  22.9 0.0 collective-permute-done.2
  22.9 0.4 collective-permute-start.6
  23.3 2.4 %collective-permute-done.3 = bf16[48,1024]{1,0:T(8,128)(2,1)S(1)} collective-permute-done((bf16[48,1024]{1,0:T(8,128)(2,1)S(1)}, bf16[48,1024]{1,0:T(8,128)(2,1)S(1)}, u32[]{:S(2)}, u32[]{:S(2)}) %collective-permute-start.3) | collective-permute-done | bytes 98336 | tf_op jit(solution)/shard_map/ppermute | solution.py:465
  25.7 1.6 %collective-permute-start.7 = (bf16[48,1024]{1,0:T(8,128)(2,1)S(1)}, bf16[48,1024]{1,0:T(8,128)(2,1)S(1)}, u32[]{:S(2)}, u32[]{:S(2)}) collective-permute-start(bf16[48,1024]{1,0:T(8,128)(2,1)S(1)} %collective-permute-done.3), channel_id=1, source_target_pairs={{0,2},{1,3},{2,0},{3,1},{4,6},{5,7},{6,4},{7,5},{8,10},{9,11},{10,... | collective-permute-start | bytes 294920 | tf_op jit(solution)/shard_map/ppermute | solution.py:466
  27.3 0.0 collective-permute-done.4
  27.3 0.0 collective-permute-done.5
  27.3 0.9 %collective-permute-done.6 = bf16[48,1024]{1,0:T(8,128)(2,1)S(1)} collective-permute-done((bf16[48,1024]{1,0:T(8,128)(2,1)S(1)}, bf16[48,1024]{1,0:T(8,128)(2,1)S(1)}, u32[]{:S(2)}, u32[]{:S(2)}) %collective-permute-start.6) | collective-permute-done | bytes 98336 | tf_op jit(solution)/shard_map/ppermute | solution.py:466
  28.3 2.1 %collective-permute-done.7 = bf16[48,1024]{1,0:T(8,128)(2,1)S(1)} collective-permute-done((bf16[48,1024]{1,0:T(8,128)(2,1)S(1)}, bf16[48,1024]{1,0:T(8,128)(2,1)S(1)}, u32[]{:S(2)}, u32[]{:S(2)}) %collective-permute-start.7) | collective-permute-done | bytes 98336 | tf_op jit(solution)/shard_map/ppermute | solution.py:466
  30.3 0.1 collective-permute-start.8
  30.4 0.0 copy-done.1
  30.5 0.1 compare_select_fusion
  30.5 1.0 %fusion.4.refs_0_ = f32[512,128]{1,0:T(8,128)S(1)} fusion(s32[128]{0:T(128)S(1)} %get-tuple-element.13, s32[128]{0:T(128)S(1)} %get-tuple-element.14, pred[128]{0:T(512)(128)(4,1)S(1)} %fusion.5), kind=kLoop, calls=%fused_computation.7 | loop fusion | flops 1048576 | bytes 263296 | tf_op jit(solution)/shard_map/jit(_where)/select_n | solution.py:445
  31.5 1.2 %collective-permute-done.8.refs_3_ = bf16[384,1024]{1,0:T(8,128)(2,1)S(1)} collective-permute-done((bf16[384,1024]{1,0:T(8,128)(2,1)S(1)}, bf16[384,1024]{1,0:T(8,128)(2,1)S(1)}, u32[]{:S(2)}, u32[]{:S(2)}) %collective-permute-start.8) | collective-permute-done | bytes 786464 | tf_op jit(solution)/shard_map/ppermute | solution.py:468
  32.7 19.6 %solve_and_filter.1 = f32[2,8,64]{2,1,0:T(8,128)} custom-call(f32[512,128]{1,0:T(8,128)S(1)} %fusion.4.refs_0_, bf16[2,64,512]{2,1,0:T(8,128)(2,1)S(1)} %get-tuple-element.11.refs_1_, bf16[384,1024]{1,0:T(8,128)(2,1)S(1)} %constant_dynamic-update-slice_fusion.refs_2_, bf16[384,1024]{1,0:T(8,128)(2,1)S(1)} %collective-permute-done.8.refs_3_), custom_call_target="tpu_custom_call" | custom-call | tf_op jit(solution)/shard_map/solve_and_filter/pallas_call | solution.py:418
  (11 shorter events, 0.1 us)
Async XLA Ops:
  0.0 13.4 %copy-start = (s32[1,48]{1,0:T(1,128)S(1)}, s32[1,48]{1,0:T(1,128)}, u32[]{:S(2)}) copy-start(s32[1,48]{1,0:T(1,128)} %refs_0_.3) | copy-start | bytes 580
  0.0 30.4 %copy-start.1 = (s32[1,8]{1,0:T(1,128)S(1)}, s32[1,8]{1,0:T(1,128)}, u32[]{:S(2)}) copy-start(s32[1,8]{1,0:T(1,128)} %param.5) | copy-start | bytes 100
  4.0 9.4 %collective-permute-start = (f32[2,64,512]{2,1,0:T(8,128)S(1)}, f32[2,64,512]{2,1,0:T(8,128)S(1)}, u32[]{:S(2)}, u32[]{:S(2)}) collective-permute-start(f32[2,64,512]{2,1,0:T(8,128)S(1)} %get-tuple-element.10), channel_id=1, source_target_pairs={{0,16},{16,0},{1,17},{17,1},{2,18},{18,2},{3,19},{19,3},{4,20},{20... | collective-permute-start | bytes 786440 | tf_op jit(solution)/shard_map/ppermute | solution.py:483
  13.6 7.6 %collective-permute-start.1 = (bf16[48,1024]{1,0:T(8,128)(2,1)S(1)}, bf16[48,1024]{1,0:T(8,128)(2,1)S(1)}, u32[]{:S(2)}, u32[]{:S(2)}) collective-permute-start(bf16[48,1024]{1,0:T(8,128)(2,1)S(1)} %get-tuple-element.12), channel_id=1, source_target_pairs={{0,4},{1,5},{2,6},{3,7},{4,8},{5,9},{6,10},{7,11},{8,12},{9,13},{1... | collective-permute-start | bytes 294920 | tf_op jit(solution)/shard_map/ppermute | solution.py:465
  15.4 7.5 %collective-permute-start.2 = (bf16[48,1024]{1,0:T(8,128)(2,1)S(1)}, bf16[48,1024]{1,0:T(8,128)(2,1)S(1)}, u32[]{:S(2)}, u32[]{:S(2)}) collective-permute-start(bf16[48,1024]{1,0:T(8,128)(2,1)S(1)} %get-tuple-element.12), channel_id=1, source_target_pairs={{0,12},{1,13},{2,14},{3,15},{4,0},{5,1},{6,2},{7,3},{8,4},{9,5},{1... | collective-permute-start | bytes 294920 | tf_op jit(solution)/shard_map/ppermute | solution.py:465
  17.5 8.2 %collective-permute-start.3 = (bf16[48,1024]{1,0:T(8,128)(2,1)S(1)}, bf16[48,1024]{1,0:T(8,128)(2,1)S(1)}, u32[]{:S(2)}, u32[]{:S(2)}) collective-permute-start(bf16[48,1024]{1,0:T(8,128)(2,1)S(1)} %get-tuple-element.12), channel_id=1, source_target_pairs={{0,8},{1,9},{2,10},{3,11},{4,12},{5,13},{6,14},{7,15},{8,0},{9,1},... | collective-permute-start | bytes 294920 | tf_op jit(solution)/shard_map/ppermute | solution.py:465
  18.5 8.8 %collective-permute-start.4 = (bf16[48,1024]{1,0:T(8,128)(2,1)S(1)}, bf16[48,1024]{1,0:T(8,128)(2,1)S(1)}, u32[]{:S(2)}, u32[]{:S(2)}) collective-permute-start(bf16[48,1024]{1,0:T(8,128)(2,1)S(1)} %get-tuple-element.12), channel_id=1, source_target_pairs={{0,2},{1,3},{2,0},{3,1},{4,6},{5,7},{6,4},{7,5},{8,10},{9,11},{10,... | collective-permute-start | bytes 294920 | tf_op jit(solution)/shard_map/ppermute | solution.py:462
  21.2 6.1 %collective-permute-start.5 = (bf16[48,1024]{1,0:T(8,128)(2,1)S(1)}, bf16[48,1024]{1,0:T(8,128)(2,1)S(1)}, u32[]{:S(2)}, u32[]{:S(2)}) collective-permute-start(bf16[48,1024]{1,0:T(8,128)(2,1)S(1)} %collective-permute-done.1), channel_id=1, source_target_pairs={{0,2},{1,3},{2,0},{3,1},{4,6},{5,7},{6,4},{7,5},{8,10},{9,11},{10,... | collective-permute-start | bytes 294920 | tf_op jit(solution)/shard_map/ppermute | solution.py:466
  22.9 5.3 %collective-permute-start.6 = (bf16[48,1024]{1,0:T(8,128)(2,1)S(1)}, bf16[48,1024]{1,0:T(8,128)(2,1)S(1)}, u32[]{:S(2)}, u32[]{:S(2)}) collective-permute-start(bf16[48,1024]{1,0:T(8,128)(2,1)S(1)} %collective-permute-done.2), channel_id=1, source_target_pairs={{0,2},{1,3},{2,0},{3,1},{4,6},{5,7},{6,4},{7,5},{8,10},{9,11},{10,... | collective-permute-start | bytes 294920 | tf_op jit(solution)/shard_map/ppermute | solution.py:466
  25.7 4.6 %collective-permute-start.7 = (bf16[48,1024]{1,0:T(8,128)(2,1)S(1)}, bf16[48,1024]{1,0:T(8,128)(2,1)S(1)}, u32[]{:S(2)}, u32[]{:S(2)}) collective-permute-start(bf16[48,1024]{1,0:T(8,128)(2,1)S(1)} %collective-permute-done.3), channel_id=1, source_target_pairs={{0,2},{1,3},{2,0},{3,1},{4,6},{5,7},{6,4},{7,5},{8,10},{9,11},{10,... | collective-permute-start | bytes 294920 | tf_op jit(solution)/shard_map/ppermute | solution.py:466
  30.3 2.4 %collective-permute-start.8 = (bf16[384,1024]{1,0:T(8,128)(2,1)S(1)}, bf16[384,1024]{1,0:T(8,128)(2,1)S(1)}, u32[]{:S(2)}, u32[]{:S(2)}) collective-permute-start(bf16[384,1024]{1,0:T(8,128)(2,1)S(1)} %constant_dynamic-update-slice_fusion.refs_2_), channel_id=1, source_target_pairs={{0,1},{1,0},{2,3},{3,2},{4,5},{5,4},{6,7},{7,6},{8,9},{9,8},{10,11... | collective-permute-start | bytes 2359304 | tf_op jit(solution)/shard_map/ppermute | solution.py:468

commit v6 on v5

--- a/solution.py
+++ b/solution.py
@@ -7,7 +7,6 @@
 from jax.experimental import pallas as pl
 from jax.experimental.pallas import tpu as pltpu
 from jax.sharding import PartitionSpec as P
-
 
 NANG = 256
 LOAD_EPS = 1e-05
@@ -37,13 +36,13 @@
     return out
 
 
-def partial_kernel(classes, dop, table, *refs):
+def partial_kernel(classes, dop, table, origin, *refs):
     cube_ref, *out_refs, buf, sems = refs
     me = lax.axis_index("dop")
     steps, _, local, step, width = buf.shape
 
     def copy(n):
-        rows = pl.ds(pl.multiple_of(n * step, step), step)
+        rows = pl.ds(pl.multiple_of(origin + n * step, step), step)
         return pltpu.make_async_copy(cube_ref.at[:, :, rows, :], buf.at[n], sems.at[n])
 
     for n in range(steps):
@@ -77,12 +76,12 @@
     lax.fori_loop(0, steps, body, 0)
 
 
-def partial_spectra(cube, table, classes, dop):
-    _, local, gates, channels = cube.shape
+def partial_spectra(cube, table, classes, dop, origin, gates):
+    _, local, _, channels = cube.shape
     step = 16
     steps = gates // step
     return pl.pallas_call(
-        lambda *refs: partial_kernel(classes, dop, table, *refs),
+        lambda *refs: partial_kernel(classes, dop, table, origin, *refs),
         in_specs=[pl.BlockSpec(memory_space=pltpu.HBM)],
         out_specs=[pl.BlockSpec(memory_space=pltpu.VMEM)] * dop,
         out_shape=[
@@ -94,11 +93,16 @@
             pltpu.SemaphoreType.DMA((steps,)),
         ],
         compiler_params=pltpu.CompilerParams(vmem_limit_bytes=52 << 20),
+        cost_estimate=pl.CostEstimate(
+            flops=4 * local * gates * channels,
+            transcendentals=0,
+            bytes_accessed=4 * local * gates * channels,
+        ),
         name="partial_spectra",
     )(cube)
 
 
-def finish_kernel(scale, *refs):
+def finish_kernel(scale, chunks, *refs):
     gates_ref, *parts, spec_ref, pack_ref = refs
     train = gates_ref.shape[1]
     gates = spec_ref.shape[1]
@@ -114,9 +118,11 @@
         cols = slice(tile * LANES, (tile + 1) * LANES)
         picked = []
         for part in range(2):
-            total = parts[0][part, :, cols]
-            for other in parts[1:]:
-                total = total + other[part, :, cols].astype(jnp.float32)
+            stretches = []
+            for chunk in range(chunks):
+                group = parts[chunk * len(parts) // chunks : (chunk + 1) * len(parts) // chunks]
+                stretches.append(tree_sum([ref[part, :, cols] for ref in group]))
+            total = stretches[0] if chunks == 1 else jnp.concatenate(stretches, 0)
             value = (total * scale).astype(jnp.bfloat16)
             spec_ref[part, :, cols] = value
             value = value.astype(jnp.float32)
@@ -129,11 +135,12 @@
         pack_ref[:, base + LANES : base + 2 * LANES] = second.astype(jnp.bfloat16)
 
 
-def finish_spectra(gate_row, parts, scale):
+def finish_spectra(gate_row, parts, chunks, scale):
     _, gates, channels = parts[0].shape
+    gates *= chunks
     train = gate_row.shape[1]
     return pl.pallas_call(
-        lambda *refs: finish_kernel(scale, *refs),
+        lambda *refs: finish_kernel(scale, chunks, *refs),
         out_shape=(
             jax.ShapeDtypeStruct((2, gates, channels), jnp.bfloat16),
             jax.ShapeDtypeStruct((train, 2 * channels), jnp.bfloat16),
@@ -299,6 +306,7 @@
     flip(0)
     norms = []
     pivot = covariance(gram(slice(0, LANES), slice(0, LANES)), True)
+    ahead = {}
     jobs = [lambda i=i: flip(i) for i in range(1, blocks)]
     jobs += [lambda j=j: fill(j, min(2, blocks - j)) for j in range(0, blocks, 2)]
     jobs.append(lambda: prepare(0))
@@ -476,12 +484,18 @@
     channels = radar_cube.shape[3]
     beams = look_angles.shape[1]
     classes = dop if local % dop == 0 else local
-    parts = partial_spectra(radar_cube, doppler_table(dop, pulses), classes, dop)
-    mine = [parts[0]]
-    for hop in range(1, dop):
-        pairs = [(d, (d + hop) % dop) for d in range(dop)]
-        mine.append(lax.ppermute(parts[hop], "dop", pairs))
-    spectrum, packed = finish_spectra(train_gates, mine, 1.0 / math.sqrt(pulses))
+    table = doppler_table(dop, pulses)
+    gates = radar_cube.shape[2]
+    chunks = 2 if gates % 32 == 0 else 1
+    chunk = gates // chunks
+    mine = []
+    for c in range(chunks):
+        parts = partial_spectra(radar_cube, table, classes, dop, c * chunk, chunk)
+        mine.append(parts[0])
+        for hop in range(1, dop):
+            pairs = [(d, (d + hop) % dop) for d in range(dop)]
+            mine.append(lax.ppermute(parts[hop], "dop", pairs))
+    spectrum, packed = finish_spectra(train_gates, mine, chunks, 1.0 / math.sqrt(pulses))
     sides = gather_rows(packed, rng)
     steer = packed_steering(look_angles[0], channels, NANG)
     out = solve_and_filter(sides, steer, spectrum, train_gates.shape[1] * rng, beams)

time: 52.4 us -> 52.1 us (level)
  waiting for transfers between devices: 14.1 us -> 12.6 us
  Pallas kernels: 23.8 us -> 25.2 us
    pallas_call x2 -> x3, Pallas kernels: 4.18 us -> 5.6 us  [the longest x2 5.42 us: partial_spectra(): pl.pallas_call(lambda *refs: partial_kernel(classes, dop, table, origin,...]
    ppermute x1 -> x2, waiting for transfers between devices: 6.31 us -> 4.95 us  [on_device(): mine.append(lax.ppermute(parts[hop], 'dop', pairs))]
    ppermute x1 -> x2, starting transfers between devices: 3.06 us -> 3.14 us  [on_device(): mine.append(lax.ppermute(parts[hop], 'dop', pairs))]
  transfers between devices with their start and end apart: 9 -> 10, of which waited for: 6 -> 7; matrix products, arithmetic and copies ran while one was open for 2% -> 2% of each run, Pallas kernels for 0% -> 5%
where the time goes in v6:
time: 52.1 us; the launch traced here: 52 us
  Pallas kernels  25.2 us (48%)
  starting transfers between devices  13 us (25%)
  waiting for transfers between devices  12.6 us (24%)
  other arithmetic  1.07 us (2%)
    pallas_call x1, Pallas kernels, solve_and_filter(): pl.pallas_call(lambda *refs: solve_kernel(train_count, beams, *refs), out...  19.6 us
    pallas_call x2, Pallas kernels, partial_spectra(): pl.pallas_call(lambda *refs: partial_kernel(classes, dop, table, origin,...  5.42 us
    ppermute x2, waiting for transfers between devices, on_device(): mine.append(lax.ppermute(parts[hop], 'dop', pairs))  4.95 us
    ppermute x3, starting transfers between devices, gather_rows(): pieces.append(lax.ppermute(rows, 'rng', shift_pairs(count, 4, outer, hop)))  4.67 us
    ppermute x3, starting transfers between devices, gather_rows(): across += [lax.ppermute(piece, 'rng', swap) for piece in pieces[1:]]  3.58 us
    ppermute x3, waiting for transfers between devices, gather_rows(): pieces.append(lax.ppermute(rows, 'rng', shift_pairs(count, 4, outer, hop)))  3.38 us
    ppermute x2, starting transfers between devices, on_device(): mine.append(lax.ppermute(parts[hop], 'dop', pairs))  3.14 us
    ppermute x3, waiting for transfers between devices, gather_rows(): across += [lax.ppermute(piece, 'rng', swap) for piece in pieces[1:]]  3.06 us
  transfers between devices with their start and end apart: 10, of which 7 were waited for; matrix products, arithmetic and copies ran while one was open for 2% of the time, Pallas kernels for 5%

profile of v6, /device:TPU:0, one launch (start us, length us, event | category | flops | bytes accessed | tf_op | source)
XLA Modules:
  0.0 52.0 jit_solution(8294343789957906701)
XLA Ops:
  0.0 0.0 copy-start
  0.0 0.0 copy-start.1
  0.0 2.7 %partial_spectra.2 = (f32[2,32,512]{2,1,0:T(8,128)S(1)}, f32[2,32,512]{2,1,0:T(8,128)S(1)}) custom-call(bf16[2,64,64,512]{3,2,1,0:T(8,128)(2,1)} %refs_0_.4), custom_call_target="tpu_custom_call" | custom-call | flops 4194304 | bytes 4194304 | tf_op jit(solution)/shard_map/partial_spectra/pallas_call | solution.py:83
  2.7 3.1 %collective-permute-start = (f32[2,32,512]{2,1,0:T(8,128)S(1)}, f32[2,32,512]{2,1,0:T(8,128)S(1)}, u32[]{:S(2)}, u32[]{:S(2)}) collective-permute-start(f32[2,32,512]{2,1,0:T(8,128)S(1)} %get-tuple-element.12), channel_id=1, source_target_pairs={{0,16},{16,0},{1,17},{17,1},{2,18},{18,2},{3,19},{19,3},{4,20},{20... | collective-permute-start | bytes 393224 | tf_op jit(solution)/shard_map/ppermute | solution.py:497
  5.8 2.7 %partial_spectra.3 = (f32[2,32,512]{2,1,0:T(8,128)S(1)}, f32[2,32,512]{2,1,0:T(8,128)S(1)}) custom-call(bf16[2,64,64,512]{3,2,1,0:T(8,128)(2,1)} %refs_0_.4), custom_call_target="tpu_custom_call" | custom-call | flops 4194304 | bytes 4194304 | tf_op jit(solution)/shard_map/partial_spectra/pallas_call | solution.py:83
  8.5 0.1 collective-permute-start.1
  8.6 0.7 %collective-permute-done.refs_2_ = f32[2,32,512]{2,1,0:T(8,128)S(1)} collective-permute-done((f32[2,32,512]{2,1,0:T(8,128)S(1)}, f32[2,32,512]{2,1,0:T(8,128)S(1)}, u32[]{:S(2)}, u32[]{:S(2)}) %collective-permute-start) | collective-permute-done | bytes 131104 | tf_op jit(solution)/shard_map/ppermute | solution.py:497
  9.3 4.2 %collective-permute-done.1.refs_4_ = f32[2,32,512]{2,1,0:T(8,128)S(1)} collective-permute-done((f32[2,32,512]{2,1,0:T(8,128)S(1)}, f32[2,32,512]{2,1,0:T(8,128)S(1)}, u32[]{:S(2)}, u32[]{:S(2)}) %collective-permute-start.1) | collective-permute-done | bytes 131104 | tf_op jit(solution)/shard_map/ppermute | solution.py:497
  13.5 0.0 copy-done
  13.5 0.2 finish_spectra.1
  13.7 1.6 %collective-permute-start.2 = (bf16[48,1024]{1,0:T(8,128)(2,1)S(1)}, bf16[48,1024]{1,0:T(8,128)(2,1)S(1)}, u32[]{:S(2)}, u32[]{:S(2)}) collective-permute-start(bf16[48,1024]{1,0:T(8,128)(2,1)S(1)} %get-tuple-element.16), channel_id=1, source_target_pairs={{0,4},{1,5},{2,6},{3,7},{4,8},{5,9},{6,10},{7,11},{8,12},{9,13},{1... | collective-permute-start | bytes 294920 | tf_op jit(solution)/shard_map/ppermute | solution.py:473
  15.4 2.2 %collective-permute-start.3 = (bf16[48,1024]{1,0:T(8,128)(2,1)S(1)}, bf16[48,1024]{1,0:T(8,128)(2,1)S(1)}, u32[]{:S(2)}, u32[]{:S(2)}) collective-permute-start(bf16[48,1024]{1,0:T(8,128)(2,1)S(1)} %get-tuple-element.16), channel_id=1, source_target_pairs={{0,12},{1,13},{2,14},{3,15},{4,0},{5,1},{6,2},{7,3},{8,4},{9,5},{1... | collective-permute-start | bytes 294920 | tf_op jit(solution)/shard_map/ppermute | solution.py:473
  17.6 0.8 %collective-permute-start.4 = (bf16[48,1024]{1,0:T(8,128)(2,1)S(1)}, bf16[48,1024]{1,0:T(8,128)(2,1)S(1)}, u32[]{:S(2)}, u32[]{:S(2)}) collective-permute-start(bf16[48,1024]{1,0:T(8,128)(2,1)S(1)} %get-tuple-element.16), channel_id=1, source_target_pairs={{0,8},{1,9},{2,10},{3,11},{4,12},{5,13},{6,14},{7,15},{8,0},{9,1},... | collective-permute-start | bytes 294920 | tf_op jit(solution)/shard_map/ppermute | solution.py:473
  18.4 1.5 %collective-permute-start.5 = (bf16[48,1024]{1,0:T(8,128)(2,1)S(1)}, bf16[48,1024]{1,0:T(8,128)(2,1)S(1)}, u32[]{:S(2)}, u32[]{:S(2)}) collective-permute-start(bf16[48,1024]{1,0:T(8,128)(2,1)S(1)} %get-tuple-element.16), channel_id=1, source_target_pairs={{0,2},{1,3},{2,0},{3,1},{4,6},{5,7},{6,4},{7,5},{8,10},{9,11},{10,... | collective-permute-start | bytes 294920 | tf_op jit(solution)/shard_map/ppermute | solution.py:470
  19.9 1.5 %collective-permute-done.2 = bf16[48,1024]{1,0:T(8,128)(2,1)S(1)} collective-permute-done((bf16[48,1024]{1,0:T(8,128)(2,1)S(1)}, bf16[48,1024]{1,0:T(8,128)(2,1)S(1)}, u32[]{:S(2)}, u32[]{:S(2)}) %collective-permute-start.2) | collective-permute-done | bytes 98336 | tf_op jit(solution)/shard_map/ppermute | solution.py:473
  21.4 1.5 %collective-permute-start.6 = (bf16[48,1024]{1,0:T(8,128)(2,1)S(1)}, bf16[48,1024]{1,0:T(8,128)(2,1)S(1)}, u32[]{:S(2)}, u32[]{:S(2)}) collective-permute-start(bf16[48,1024]{1,0:T(8,128)(2,1)S(1)} %collective-permute-done.2), channel_id=1, source_target_pairs={{0,2},{1,3},{2,0},{3,1},{4,6},{5,7},{6,4},{7,5},{8,10},{9,11},{10,... | collective-permute-start | bytes 294920 | tf_op jit(solution)/shard_map/ppermute | solution.py:474
  22.9 0.0 collective-permute-done.3
  22.9 0.6 %collective-permute-start.7 = (bf16[48,1024]{1,0:T(8,128)(2,1)S(1)}, bf16[48,1024]{1,0:T(8,128)(2,1)S(1)}, u32[]{:S(2)}, u32[]{:S(2)}) collective-permute-start(bf16[48,1024]{1,0:T(8,128)(2,1)S(1)} %collective-permute-done.3), channel_id=1, source_target_pairs={{0,2},{1,3},{2,0},{3,1},{4,6},{5,7},{6,4},{7,5},{8,10},{9,11},{10,... | collective-permute-start | bytes 294920 | tf_op jit(solution)/shard_map/ppermute | solution.py:474
  23.5 1.9 %collective-permute-done.4 = bf16[48,1024]{1,0:T(8,128)(2,1)S(1)} collective-permute-done((bf16[48,1024]{1,0:T(8,128)(2,1)S(1)}, bf16[48,1024]{1,0:T(8,128)(2,1)S(1)}, u32[]{:S(2)}, u32[]{:S(2)}) %collective-permute-start.4) | collective-permute-done | bytes 98336 | tf_op jit(solution)/shard_map/ppermute | solution.py:473
  25.4 1.5 %collective-permute-start.8 = (bf16[48,1024]{1,0:T(8,128)(2,1)S(1)}, bf16[48,1024]{1,0:T(8,128)(2,1)S(1)}, u32[]{:S(2)}, u32[]{:S(2)}) collective-permute-start(bf16[48,1024]{1,0:T(8,128)(2,1)S(1)} %collective-permute-done.4), channel_id=1, source_target_pairs={{0,2},{1,3},{2,0},{3,1},{4,6},{5,7},{6,4},{7,5},{8,10},{9,11},{10,... | collective-permute-start | bytes 294920 | tf_op jit(solution)/shard_map/ppermute | solution.py:474
  26.9 0.0 collective-permute-done.5
  26.9 0.0 collective-permute-done.6
  26.9 1.6 %collective-permute-done.7 = bf16[48,1024]{1,0:T(8,128)(2,1)S(1)} collective-permute-done((bf16[48,1024]{1,0:T(8,128)(2,1)S(1)}, bf16[48,1024]{1,0:T(8,128)(2,1)S(1)}, u32[]{:S(2)}, u32[]{:S(2)}) %collective-permute-start.7) | collective-permute-done | bytes 98336 | tf_op jit(solution)/shard_map/ppermute | solution.py:474
  28.5 1.5 %collective-permute-done.8 = bf16[48,1024]{1,0:T(8,128)(2,1)S(1)} collective-permute-done((bf16[48,1024]{1,0:T(8,128)(2,1)S(1)}, bf16[48,1024]{1,0:T(8,128)(2,1)S(1)}, u32[]{:S(2)}, u32[]{:S(2)}) %collective-permute-start.8) | collective-permute-done | bytes 98336 | tf_op jit(solution)/shard_map/ppermute | solution.py:474
  30.0 0.1 collective-permute-start.9
  30.1 0.0 copy-done.1
  30.1 0.1 compare_select_fusion
  30.2 1.0 %fusion.4.refs_0_ = f32[512,128]{1,0:T(8,128)S(1)} fusion(s32[128]{0:T(128)S(1)} %get-tuple-element.17, s32[128]{0:T(128)S(1)} %get-tuple-element.18, pred[128]{0:T(512)(128)(4,1)S(1)} %fusion.5), kind=kLoop, calls=%fused_computation.7 | loop fusion | flops 1048576 | bytes 263296 | tf_op jit(solution)/shard_map/jit(_where)/select_n | solution.py:453
  31.2 1.2 %collective-permute-done.9.refs_3_ = bf16[384,1024]{1,0:T(8,128)(2,1)S(1)} collective-permute-done((bf16[384,1024]{1,0:T(8,128)(2,1)S(1)}, bf16[384,1024]{1,0:T(8,128)(2,1)S(1)}, u32[]{:S(2)}, u32[]{:S(2)}) %collective-permute-start.9) | collective-permute-done | bytes 786464 | tf_op jit(solution)/shard_map/ppermute | solution.py:476
  32.4 19.6 %solve_and_filter.1 = f32[2,8,64]{2,1,0:T(8,128)} custom-call(f32[512,128]{1,0:T(8,128)S(1)} %fusion.4.refs_0_, bf16[2,64,512]{2,1,0:T(8,128)(2,1)S(1)} %get-tuple-element.15.refs_1_, bf16[384,1024]{1,0:T(8,128)(2,1)S(1)} %constant_dynamic-update-slice_fusion.refs_2_, bf16[384,1024]{1,0:T(8,128)(2,1)S(1)} %collective-permute-done.9.refs_3_), custom_call_target="tpu_custom_call" | custom-call | tf_op jit(solution)/shard_map/solve_and_filter/pallas_call | solution.py:426
  (11 shorter events, 0.1 us)
Async XLA Ops:
  0.0 13.5 %copy-start = (s32[1,48]{1,0:T(1,128)S(1)}, s32[1,48]{1,0:T(1,128)}, u32[]{:S(2)}) copy-start(s32[1,48]{1,0:T(1,128)} %refs_0_.5) | copy-start | bytes 580
  0.0 30.1 %copy-start.1 = (s32[1,8]{1,0:T(1,128)S(1)}, s32[1,8]{1,0:T(1,128)}, u32[]{:S(2)}) copy-start(s32[1,8]{1,0:T(1,128)} %param.5) | copy-start | bytes 100
  2.7 6.6 %collective-permute-start = (f32[2,32,512]{2,1,0:T(8,128)S(1)}, f32[2,32,512]{2,1,0:T(8,128)S(1)}, u32[]{:S(2)}, u32[]{:S(2)}) collective-permute-start(f32[2,32,512]{2,1,0:T(8,128)S(1)} %get-tuple-element.12), channel_id=1, source_target_pairs={{0,16},{16,0},{1,17},{17,1},{2,18},{18,2},{3,19},{19,3},{4,20},{20... | collective-permute-start | bytes 393224 | tf_op jit(solution)/shard_map/ppermute | solution.py:497
  8.5 5.0 %collective-permute-start.1 = (f32[2,32,512]{2,1,0:T(8,128)S(1)}, f32[2,32,512]{2,1,0:T(8,128)S(1)}, u32[]{:S(2)}, u32[]{:S(2)}) collective-permute-start(f32[2,32,512]{2,1,0:T(8,128)S(1)} %get-tuple-element.14), channel_id=1, source_target_pairs={{0,16},{16,0},{1,17},{17,1},{2,18},{18,2},{3,19},{19,3},{4,20},{20... | collective-permute-start | bytes 393224 | tf_op jit(solution)/shard_map/ppermute | solution.py:497
  13.7 7.6 %collective-permute-start.2 = (bf16[48,1024]{1,0:T(8,128)(2,1)S(1)}, bf16[48,1024]{1,0:T(8,128)(2,1)S(1)}, u32[]{:S(2)}, u32[]{:S(2)}) collective-permute-start(bf16[48,1024]{1,0:T(8,128)(2,1)S(1)} %get-tuple-element.16), channel_id=1, source_target_pairs={{0,4},{1,5},{2,6},{3,7},{4,8},{5,9},{6,10},{7,11},{8,12},{9,13},{1... | collective-permute-start | bytes 294920 | tf_op jit(solution)/shard_map/ppermute | solution.py:473
  15.4 7.5 %collective-permute-start.3 = (bf16[48,1024]{1,0:T(8,128)(2,1)S(1)}, bf16[48,1024]{1,0:T(8,128)(2,1)S(1)}, u32[]{:S(2)}, u32[]{:S(2)}) collective-permute-start(bf16[48,1024]{1,0:T(8,128)(2,1)S(1)} %get-tuple-element.16), channel_id=1, source_target_pairs={{0,12},{1,13},{2,14},{3,15},{4,0},{5,1},{6,2},{7,3},{8,4},{9,5},{1... | collective-permute-start | bytes 294920 | tf_op jit(solution)/shard_map/ppermute | solution.py:473
  17.6 7.8 %collective-permute-start.4 = (bf16[48,1024]{1,0:T(8,128)(2,1)S(1)}, bf16[48,1024]{1,0:T(8,128)(2,1)S(1)}, u32[]{:S(2)}, u32[]{:S(2)}) collective-permute-start(bf16[48,1024]{1,0:T(8,128)(2,1)S(1)} %get-tuple-element.16), channel_id=1, source_target_pairs={{0,8},{1,9},{2,10},{3,11},{4,12},{5,13},{6,14},{7,15},{8,0},{9,1},... | collective-permute-start | bytes 294920 | tf_op jit(solution)/shard_map/ppermute | solution.py:473
  18.4 8.5 %collective-permute-start.5 = (bf16[48,1024]{1,0:T(8,128)(2,1)S(1)}, bf16[48,1024]{1,0:T(8,128)(2,1)S(1)}, u32[]{:S(2)}, u32[]{:S(2)}) collective-permute-start(bf16[48,1024]{1,0:T(8,128)(2,1)S(1)} %get-tuple-element.16), channel_id=1, source_target_pairs={{0,2},{1,3},{2,0},{3,1},{4,6},{5,7},{6,4},{7,5},{8,10},{9,11},{10,... | collective-permute-start | bytes 294920 | tf_op jit(solution)/shard_map/ppermute | solution.py:470
  21.4 5.6 %collective-permute-start.6 = (bf16[48,1024]{1,0:T(8,128)(2,1)S(1)}, bf16[48,1024]{1,0:T(8,128)(2,1)S(1)}, u32[]{:S(2)}, u32[]{:S(2)}) collective-permute-start(bf16[48,1024]{1,0:T(8,128)(2,1)S(1)} %collective-permute-done.2), channel_id=1, source_target_pairs={{0,2},{1,3},{2,0},{3,1},{4,6},{5,7},{6,4},{7,5},{8,10},{9,11},{10,... | collective-permute-start | bytes 294920 | tf_op jit(solution)/shard_map/ppermute | solution.py:474
  22.9 5.7 %collective-permute-start.7 = (bf16[48,1024]{1,0:T(8,128)(2,1)S(1)}, bf16[48,1024]{1,0:T(8,128)(2,1)S(1)}, u32[]{:S(2)}, u32[]{:S(2)}) collective-permute-start(bf16[48,1024]{1,0:T(8,128)(2,1)S(1)} %collective-permute-done.3), channel_id=1, source_target_pairs={{0,2},{1,3},{2,0},{3,1},{4,6},{5,7},{6,4},{7,5},{8,10},{9,11},{10,... | collective-permute-start | bytes 294920 | tf_op jit(solution)/shard_map/ppermute | solution.py:474
  25.4 4.6 %collective-permute-start.8 = (bf16[48,1024]{1,0:T(8,128)(2,1)S(1)}, bf16[48,1024]{1,0:T(8,128)(2,1)S(1)}, u32[]{:S(2)}, u32[]{:S(2)}) collective-permute-start(bf16[48,1024]{1,0:T(8,128)(2,1)S(1)} %collective-permute-done.4), channel_id=1, source_target_pairs={{0,2},{1,3},{2,0},{3,1},{4,6},{5,7},{6,4},{7,5},{8,10},{9,11},{10,... | collective-permute-start | bytes 294920 | tf_op jit(solution)/shard_map/ppermute | solution.py:474
  30.0 2.4 %collective-permute-start.9 = (bf16[384,1024]{1,0:T(8,128)(2,1)S(1)}, bf16[384,1024]{1,0:T(8,128)(2,1)S(1)}, u32[]{:S(2)}, u32[]{:S(2)}) collective-permute-start(bf16[384,1024]{1,0:T(8,128)(2,1)S(1)} %constant_dynamic-update-slice_fusion.refs_2_), channel_id=1, source_target_pairs={{0,1},{1,0},{2,3},{3,2},{4,5},{5,4},{6,7},{7,6},{8,9},{9,8},{10,11... | collective-permute-start | bytes 2359304 | tf_op jit(solution)/shard_map/ppermute | solution.py:476
